TPU v7x, 256 devices: a whole 4x4x8 slice. The times are simulated.
256 devices in a mesh: section: 4 (over z_hi), seq: 64 (over x, y, z_lo, core).
Axes of the slice: x: 4, y: 4, z: 8 (z_hi: 4, z_lo: 2; z = z_hi * 2 + z_lo), core: 2. Of those that a mesh axis runs over, the one named last changes fastest.
Arguments:
- memory: bfloat16 [8, 4096, 4096], P(None, 'seq', 'section'), may hold values from -6 to 6
- kv_weight: bfloat16 [4096, 4096], P('seq', 'section'), may hold values from -0.09375 to 0.09375
- mem_lengths: int32 [8], replicated, may hold values from 1024 to 4096, as said below
- queries: bfloat16 [16384, 2048], P('seq', 'section'), may hold values from -128 to 128
- out_weight: bfloat16 [2048, 4096], P('section'), may hold values from -0.125 to 0.125
- residual: bfloat16 [16384, 4096], P(('seq', 'section')), may hold values from -1.5 to 1.5
- norm_gain: float32 [4096], replicated, may hold values from 0.5 to 1.5
Outputs:
- hidden_out: bfloat16 [16384, 4096], P(('seq', 'section'))
- normed_out: bfloat16 [16384, 4096], P(('seq', 'section'))
Inputs may be any that keep to these rules, and one draw needn't show every extreme that they name: `mem_lengths`: valid memory positions of each proof state; positions at or beyond it are padding; at least one proof state has none.
All inputs are finite; a program needn't handle non-finite values.
Results may differ from a plain program's by a relative error of at most 0.012.
Values may be sent and summed in bfloat16 or wider, within the bound.
No kernel may reach another device: no remote copies, remote signals or barrier semaphores. Data moves between devices by JAX's collectives and lax.ppermute only.
A program may use at most 128 MiB of HBM per device.

v0:
```python
import functools
import math

import jax
import jax.numpy as jnp
from jax import lax
from jax.experimental import pallas as pl
from jax.experimental.pallas import tpu as pltpu
from jax.sharding import Mesh, PartitionSpec as P


DH = 256
CHUNKS = 2
BF = jnp.bfloat16
F32 = jnp.float32
X = "x"
XY = ("x", "yh", "yl")
Z = "zh"
EXP_SCALE = math.log2(math.e) / math.sqrt(DH)
FWD = [(i, (i + 1) % 4) for i in range(4)]
BWD = [(i, (i + 3) % 4) for i in range(4)]


def swap(a, axis):
    return lax.ppermute(a, axis, [(0, 1), (1, 0)])


def pair(a, b, index, axis=0):
    return jnp.where(index == 0, jnp.concatenate([a, b], axis), jnp.concatenate([b, a], axis))


def pick(a, b, index):
    return jnp.where(index == 0, a, b)


def project_kernel(where_ref, own, nxt, opp_a, opp_b, prev, w_mine, w_theirs, out_ref, buf, sem):
    zh, c = where_ref[0], where_ref[3]
    copies = []
    for dz in range(4):
        block = pl.ds(pl.multiple_of(lax.rem(zh + dz, 4) * 1024, 1024), 1024)
        for j, w in enumerate((w_mine, w_theirs)):
            copies.append(pltpu.make_async_copy(w.at[block], buf.at[2 * dz + j], sem.at[2 * dz + j]))
            copies[-1].start()
    acc = [jnp.zeros((own.shape[0], 2 * DH), F32)] * 2
    for dz in range(4):
        if dz == 2:
            rows = jnp.concatenate([opp_a[...], opp_b[...]], 0)
        else:
            rows = (own, nxt, None, prev)[dz][...]
        for j in range(2):
            copies[2 * dz + j].wait()
            acc[j] = acc[j] + jnp.dot(rows, buf[2 * dz + j], preferred_element_type=F32)
    shape = (out_ref.shape[0],) + out_ref.shape[2:]
    out_ref[:, c] = acc[0].astype(BF).reshape(shape)
    out_ref[:, 1 - c] = acc[1].astype(BF).reshape(shape)


def project(where, pieces, weights):
    rows = pieces[0].shape[0]
    vmem = pl.BlockSpec(memory_space=pltpu.VMEM)
    return pl.pallas_call(
        project_kernel,
        out_shape=jax.ShapeDtypeStruct((8, 2, rows // 8, 2 * DH), BF),
        in_specs=[pl.BlockSpec(memory_space=pltpu.SMEM)] + [vmem] * 5 + [pl.BlockSpec(memory_space=pl.ANY)] * 2,
        out_specs=vmem,
        scratch_shapes=[pltpu.VMEM((8, 1024, 2 * DH), BF), pltpu.SemaphoreType.DMA((8,))],
        name="project",
    )(where, *pieces, *weights)


def attend_kernel(chunk_rows, where_ref, q_ref, *refs):
    kv_refs, out_ref, bias_ref, vt_ref = refs[:-3], refs[-3], refs[-2], refs[-1]
    length, base = where_ref[0], where_ref[1]
    per = chunk_rows // 16

    @pl.when(pl.program_id(0) == 0)
    def _():
        for j in range(len(kv_refs)):
            row = lax.broadcasted_iota(jnp.int32, (chunk_rows, 128), 0)
            source = row // (2 * per)
            side = (row // per) % 2
            position = source * 512 + base + side * 64 + j * per + row % per
            bias_ref[pl.ds(j * chunk_rows, chunk_rows), :] = jnp.where(position < length, 0.0, -1e30)
            vt_ref[j] = kv_refs[j][:, DH:].T

    q = q_ref[...]
    scores = []
    for j, kv in enumerate(kv_refs):
        s = lax.dot_general(kv[:, :DH], q, (((1,), (1,)), ((), ())), preferred_element_type=F32)
        bias = bias_ref[pl.ds(j * chunk_rows, chunk_rows), :]
        scores.append(s + jnp.concatenate([bias] * (q.shape[0] // 128), axis=1))
    high = functools.reduce(jnp.maximum, [jnp.max(s, axis=0, keepdims=True) for s in scores])
    total = jnp.zeros_like(high)
    acc = jnp.zeros((DH, q.shape[0]), F32)
    for j, s in enumerate(scores):
        p = jnp.exp2((s - high) * EXP_SCALE)
        total += jnp.sum(p, axis=0, keepdims=True)
        acc += jnp.dot(vt_ref[j], p.astype(BF), preferred_element_type=F32)
    out_ref[0, :DH] = (acc / total).astype(BF)
    lse = high * EXP_SCALE + jnp.log2(total)
    first = lse.astype(BF)
    rest = lse - first.astype(F32)
    second = rest.astype(BF)
    third = (rest - second.astype(F32)).astype(BF)
    zero = jnp.zeros((13, q.shape[0]), F32)
    stats = jnp.concatenate([first.astype(F32), second.astype(F32), third.astype(F32), zero], 0)
    out_ref[0, DH:] = stats.astype(BF)


def attend(where, q, kvs):
    rows = kvs[0].shape[0]
    tokens = q.shape[0]
    whole = pl.BlockSpec((rows, 2 * DH), lambda i: (0, 0))
    return pl.pallas_call(
        functools.partial(attend_kernel, rows),
        grid=(tokens // 256,),
        out_shape=jax.ShapeDtypeStruct((tokens // 256, DH + 16, 256), BF),
        in_specs=[pl.BlockSpec(memory_space=pltpu.SMEM), pl.BlockSpec((256, DH), lambda i: (i, 0))] + [whole] * len(kvs),
        out_specs=pl.BlockSpec((1, DH + 16, 256), lambda i: (i, 0, 0)),
        scratch_shapes=[pltpu.VMEM((rows * len(kvs), 128), F32), pltpu.VMEM((len(kvs), DH, rows), BF)],
        name="attend",
    )(where, q, *kvs)


def merge_kernel(a_ref, b_ref, c_ref, d_ref, out_ref):
    refs = (a_ref, b_ref, c_ref, d_ref)
    for side in range(2):
        stats = [ref[side, DH:].astype(F32) for ref in refs]
        lse = [s[0:1] + s[1:2] + s[2:3] for s in stats]
        high = functools.reduce(jnp.maximum, lse)
        weight = [jnp.exp2(v - high) for v in lse]
        inverse = 1.0 / sum(weight)
        context = sum(ref[side, :DH].astype(F32) * (w * inverse) for ref, w in zip(refs, weight))
        out_ref[side] = context.T.astype(BF)


def merge(parts):
    vmem = pl.BlockSpec(memory_space=pltpu.VMEM)
    return pl.pallas_call(
        merge_kernel,
        out_shape=jax.ShapeDtypeStruct((2, 256, DH), BF),
        in_specs=[vmem] * 4,
        out_specs=vmem,
        name="merge",
    )(*parts)


def output_kernel(where_ref, *refs):
    ctx, w_ref, out_own, out_oth, acc = refs[:8], refs[8], refs[9], refs[10], refs[11]
    k = pl.program_id(0)

    @pl.when(k == 0)
    def _():
        acc[...] = jnp.zeros_like(acc)

    rows = jnp.concatenate([ctx[0][...], ctx[1][...]], 0)
    for dz in range(1, 4):
        rows = jnp.where(k == dz, jnp.concatenate([ctx[2 * dz][...], ctx[2 * dz + 1][...]], 0), rows)
    acc[...] += jnp.dot(rows, w_ref[...], preferred_element_type=F32)

    @pl.when(k == 3)
    def _():
        out_own[...] = acc[:64]
        out_oth[...] = acc[64:]


def output(where, ctx, w):
    whole = pl.BlockSpec((64, 2 * DH), lambda i: (0, 0))
    out = pl.BlockSpec((64, 2048), lambda i: (0, 0))
    return pl.pallas_call(
        output_kernel,
        grid=(4,),
        out_shape=[jax.ShapeDtypeStruct((64, 2048), F32)] * 2,
        in_specs=[pl.BlockSpec(memory_space=pltpu.SMEM)] + [whole] * 8 + [pl.BlockSpec((512, 2048), lambda i: (i, 0))],
        out_specs=[out] * 2,
        scratch_shapes=[pltpu.VMEM((128, 2048), F32)],
        name="output",
    )(where, *ctx, w)


def finish_kernel(c_ref, mine, other, residual, gain, hidden, normed):
    swapped = c_ref[0] == 1
    a, b = mine[...], other[...]
    low = residual[:, :2048].astype(F32) + jnp.where(swapped, b, a)
    high = residual[:, 2048:].astype(F32) + jnp.where(swapped, a, b)
    squares = jnp.sum(low * low, -1, keepdims=True) + jnp.sum(high * high, -1, keepdims=True)
    scale = lax.rsqrt(squares * (1.0 / 4096) + 1e-06)
    hidden[:, :2048] = low.astype(BF)
    hidden[:, 2048:] = high.astype(BF)
    normed[:, :2048] = (low * scale * gain[:, :2048]).astype(BF)
    normed[:, 2048:] = (high * scale * gain[:, 2048:]).astype(BF)


def finish(core, mine, other, residual, gain):
    vmem = pl.BlockSpec(memory_space=pltpu.VMEM)
    return pl.pallas_call(
        finish_kernel,
        out_shape=[jax.ShapeDtypeStruct(residual.shape, BF)] * 2,
        in_specs=[pl.BlockSpec(memory_space=pltpu.SMEM)] + [vmem] * 4,
        out_specs=[vmem] * 2,
        name="finish",
    )(core, mine, other, residual, gain)


def shards(memory, kv_weight, mem_lengths, queries, out_weight, residual, norm_gain):
    zh, x, yh, yl, zl, c = (lax.axis_index(a) for a in (Z, X, "yh", "yl", "zl", "c"))
    y = yh * 2 + yl
    where = jnp.stack([zh, x, y, c]).astype(jnp.int32)

    mine = pick(kv_weight[:, :512], kv_weight[:, 512:], c)
    theirs = pick(kv_weight[:, 512:], kv_weight[:, :512], c)
    w_c = swap(theirs, "c")
    w_z = swap(mine, "zl")
    w_zc = lax.ppermute(theirs, ("zl", "c"), [(i, 3 - i) for i in range(4)])
    rows = pair(pair(mine, w_c, c), pair(w_z, w_zc, c), zl)
    w_mine = lax.all_gather(rows, XY, axis=0, tiled=True)

    step = memory.shape[1] // CHUNKS
    half = 4 * step
    chunks = []
    for j in range(CHUNKS):
        own = memory[:, j * step : (j + 1) * step].reshape(8 * step, 1024)
        prev = lax.ppermute(own, Z, FWD)
        nxt = lax.ppermute(own, Z, BWD)
        opp_a = lax.ppermute(prev[:half], Z, FWD)
        opp_b = lax.ppermute(nxt[half:], Z, BWD)
        chunks.append([own, nxt, opp_a, opp_b, prev])

    ow = lax.dynamic_slice(out_weight, (0, c * 2048 + (x * 4 + y) * 128), (512, 128))
    ow = [ow] + [lax.ppermute(ow, Z, [(i, (i + 4 - d) % 4) for i in range(4)]) for d in (1, 2, 3)]
    ow = jnp.concatenate(ow, 0)

    w_mine, ow = lax.optimization_barrier((w_mine, ow))
    ow = lax.all_gather(ow, XY, axis=1, tiled=True)
    w_theirs = swap(w_mine, "c")

    kvs = []
    for pieces in chunks:
        both = project(where, pieces, (w_mine, w_theirs))
        both = lax.all_to_all(both.reshape(16, step, 512), (X, "yh", "c"), 0, 0, tiled=True)
        kvs.append(both.reshape(16 * step, 512))

    other = pick(queries[:, DH:], queries[:, :DH], c)
    other = swap(other, "c")
    q = pair(pick(queries[:, :DH], queries[:, DH:], c), other, c)
    q = pair(q, swap(q, "zl"), zl)
    q = pair(q, swap(q, "yl"), yl)

    length = lax.dynamic_index_in_dim(mem_lengths, x * 2 + yh, 0, keepdims=False)
    here = jnp.stack([length, yl * 256 + zl * 128]).astype(jnp.int32)
    part = attend(here, q, kvs).reshape(2, 2, 2, DH + 16, 256)

    def tokens_of(dy, dz):
        return lax.dynamic_slice(part, (yl ^ dy, zl ^ dz, 0, 0, 0), (1, 1) + part.shape[2:])[0, 0]

    both_swap = [(i, 3 - i) for i in range(4)]
    parts = (
        tokens_of(0, 0),
        swap(tokens_of(1, 0), "yl"),
        swap(tokens_of(0, 1), "zl"),
        lax.ppermute(tokens_of(1, 1), ("yl", "zl"), both_swap),
    )
    head = merge(parts)
    other = swap(pick(head[1], head[0], c), "c")
    mine = pick(head[0], head[1], c)
    context = pair(mine, other, c, 1).reshape(4, 64, 512)

    def section(d):
        return lax.dynamic_index_in_dim(context, (zh + d) % 4, 0, keepdims=False)

    near = [section(0)] + [lax.ppermute(section(4 - d), Z, [(i, (i + 4 - d) % 4) for i in range(4)]) for d in (1, 2, 3)]
    ctx = []
    for a in near:
        ctx += [a, swap(a, "c")]
    mine, theirs = output(where, ctx, ow)
    other = swap(theirs, "c")
    return tuple(finish(c.reshape(1).astype(jnp.int32), mine, other, residual, norm_gain.reshape(1, -1)))


def solution(mesh):
    fine = Mesh(mesh.devices.reshape(4, 4, 2, 2, 2, 2), (Z, X, "yh", "yl", "zl", "c"))
    seq = (X, "yh", "yl", "zl", "c")
    in_specs = (
        P(None, seq, Z),
        P(seq, Z),
        P(),
        P(seq, Z),
        P(Z, None),
        P(seq + (Z,), None),
        P(),
    )
    out_specs = (P(seq + (Z,), None), P(seq + (Z,), None))
    return jax.shard_map(shards, mesh=fine, in_specs=in_specs, out_specs=out_specs, check_vma=False)
```

profile of v0, /device:TPU:1, one launch (start us, length us, event | category | flops | bytes accessed | tf_op | source)
XLA Modules:
  0.0 270.7 jit_solution(503108556430306853)
XLA Ops:
  7.2 1.0 broadcast_select_fusion.4
  8.2 3.3 %collective-permute-start.7 = (bf16[64,512]{1,0:T(8,128)(2,1)S(1)}, bf16[64,512]{1,0:T(8,128)(2,1)S(1)}, u32[]{:S(2)}, u32[]{:S(2)}) collective-permute-start(bf16[64,512]{1,0:T(8,128)(2,1)S(1)} %get-tuple-element.25), channel_id=1, source_target_pairs={{0,1},{1,0},{2,3},{3,2},{4,5},{5,4},{6,7},{7,6},{8,9},{9,8},{10,11... | collective-permute-start | bytes 196616 | tf_op jit(solution)/shard_map/ppermute | solution.py:25
  11.5 1.4 collective-permute-start.8
  13.0 3.4 %collective-permute-done.8 = bf16[64,512]{1,0:T(8,128)(2,1)S(1)} collective-permute-done((bf16[64,512]{1,0:T(8,128)(2,1)S(1)}, bf16[64,512]{1,0:T(8,128)(2,1)S(1)}, u32[]{:S(2)}, u32[]{:S(2)}) %collective-permute-start.8) | collective-permute-done | bytes 65568 | tf_op jit(solution)/shard_map/ppermute | solution.py:25
  18.2 4.4 %collective-permute-start.10 = (bf16[512,128]{1,0:T(8,128)(2,1)S(1)}, bf16[512,128]{1,0:T(8,128)(2,1)S(1)}, u32[]{:S(2)}, u32[]{:S(2)}) collective-permute-start(bf16[512,128]{1,0:T(8,128)(2,1)S(1)} %constant_dynamic-slice_fusion), channel_id=1, source_target_pairs={{0,192},{64,0},{128,64},{192,128},{1,193},{65,1},{129,65},{193,129... | collective-permute-start | bytes 393224 | tf_op jit(solution)/shard_map/ppermute | solution.py:230
  22.6 1.0 collective-permute-start.11
  23.6 2.3 collective-permute-start.12
  25.9 1.3 collective-permute-done.10
  27.1 6.4 %collective-permute-done.11 = bf16[512,128]{1,0:T(8,128)(2,1)S(1)} collective-permute-done((bf16[512,128]{1,0:T(8,128)(2,1)S(1)}, bf16[512,128]{1,0:T(8,128)(2,1)S(1)}, u32[]{:S(2)}, u32[]{:S(2)}) %collective-permute-start.11) | collective-permute-done | bytes 131104 | tf_op jit(solution)/shard_map/ppermute | solution.py:230
  34.4 40.8 %all-gather.3.cloned.1.call-done.w_mine = bf16[4096,512]{1,0:T(8,128)(2,1)} async-done(((bf16[256,512]{1,0:T(8,128)(2,1)}), bf16[4096,512]{1,0:T(8,128)(2,1)}) %all-gather.3.cloned.1.call-update) | async-done | bytes 4194320 | tf_op jit(solution)/shard_map/all_gather | solution.py:216
  76.3 2.3 collective-permute-start.15
  78.6 1.7 collective-permute-start.14
  80.3 19.5 %collective-permute-done.15.prev = bf16[256,1024]{1,0:T(8,128)(2,1)S(1)} collective-permute-done((bf16[256,1024]{1,0:T(8,128)(2,1)S(1)}, bf16[256,1024]{1,0:T(8,128)(2,1)S(1)}, u32[]{:S(2)}, u32[]{:S(2)}) %collective-permute-start.15) | collective-permute-done | bytes 524320 | tf_op jit(solution)/shard_map/ppermute | solution.py:223
  99.8 4.8 %collective-permute-start.16 = (bf16[128,1024]{1,0:T(8,128)(2,1)S(1)}, bf16[128,1024]{1,0:T(8,128)(2,1)}, u32[]{:S(2)}, u32[]{:S(2)}) collective-permute-start(bf16[128,1024]{1,0:T(8,128)(2,1)S(1)} %slice.56), channel_id=1, source_target_pairs={{0,64},{64,128},{128,192},{192,0},{1,65},{65,129},{129,193},{193,1... | collective-permute-start | bytes 786440 | tf_op jit(solution)/shard_map/ppermute | solution.py:225
  104.6 1.3 collective-permute-start
  105.9 4.3 %collective-permute-start.4 = (bf16[256,1024]{1,0:T(8,128)(2,1)S(1)}, bf16[256,1024]{1,0:T(8,128)(2,1)S(1)}, u32[]{:S(2)}, u32[]{:S(2)}) collective-permute-start(bf16[256,1024]{1,0:T(8,128)(2,1)S(1)} %bitcast.36), channel_id=1, source_target_pairs={{0,64},{64,128},{128,192},{192,0},{1,65},{65,129},{129,193},{193,1... | collective-permute-start | bytes 1572872 | tf_op jit(solution)/shard_map/ppermute | solution.py:223
  111.1 4.5 %collective-permute-done.16.opp_a = bf16[128,1024]{1,0:T(8,128)(2,1)} collective-permute-done((bf16[128,1024]{1,0:T(8,128)(2,1)S(1)}, bf16[128,1024]{1,0:T(8,128)(2,1)}, u32[]{:S(2)}, u32[]{:S(2)}) %collective-permute-start.16) | collective-permute-done | bytes 262176 | tf_op jit(solution)/shard_map/ppermute | solution.py:225
  115.6 1.7 collective-permute-start.1
  118.0 28.6 %collective-permute-done.17.opp_b = bf16[128,1024]{1,0:T(8,128)(2,1)} collective-permute-done((bf16[128,1024]{1,0:T(8,128)(2,1)}, bf16[128,1024]{1,0:T(8,128)(2,1)}, u32[]{:S(2)}, u32[]{:S(2)}) %collective-permute-start.17) | collective-permute-done | bytes 262176 | tf_op jit(solution)/shard_map/ppermute | solution.py:226
  146.6 7.3 %project.3 = bf16[8,2,32,512]{3,2,1,0:T(8,128)(2,1)} custom-call(s32[4]{0:T(128)} %pad_add_fusion.where_ref, bf16[256,1024]{1,0:T(8,128)(2,1)} %bitcast.41, bf16[256,1024]{1,0:T(8,128)(2,1)} %copy-done.7, bf16[128,1024]{1,0:T(8,128)(2,1)} %collective-permute-done.16.opp_a, bf16[128,1024]{1,0:T(8,128)(2,1)} %collective-permute-done.17.opp_b, ...), custom_call_target="tpu_custom_call" | custom-call | tf_op jit(solution)/shard_map/project/pallas_call | solution.py:61
  153.9 5.8 %all-to-all-start.1 = ((bf16[16,32,512]{2,1,0:T(8,128)(2,1)}), bf16[16,32,512]{2,1,0:T(8,128)(2,1)S(1)}, u32[]{:S(2)}, u32[]{:S(2)}) async-start(bf16[16,32,512]{2,1,0:T(8,128)(2,1)} %bitcast.35), calls=%async_computation.1 | async-start | bytes 1048576 | tf_op jit(solution)/shard_map/all_to_all | solution.py:240
  159.6 1.2 maximum_select_fusion.1
  161.1 2.1 collective-permute-start.5
  163.3 1.6 collective-permute-start.6
  164.9 5.9 %collective-permute-done.5.opp_a = bf16[128,1024]{1,0:T(8,128)(2,1)S(1)} collective-permute-done((bf16[128,1024]{1,0:T(8,128)(2,1)S(1)}, bf16[128,1024]{1,0:T(8,128)(2,1)S(1)}, u32[]{:S(2)}, u32[]{:S(2)}) %collective-permute-start.5) | collective-permute-done | bytes 262176 | tf_op jit(solution)/shard_map/ppermute | solution.py:225
  170.8 3.8 %collective-permute-done.6.opp_b = bf16[128,1024]{1,0:T(8,128)(2,1)S(1)} collective-permute-done((bf16[128,1024]{1,0:T(8,128)(2,1)S(1)}, bf16[128,1024]{1,0:T(8,128)(2,1)S(1)}, u32[]{:S(2)}, u32[]{:S(2)}) %collective-permute-start.6) | collective-permute-done | bytes 262176 | tf_op jit(solution)/shard_map/ppermute | solution.py:226
  175.3 7.0 %project.2 = bf16[8,2,32,512]{3,2,1,0:T(8,128)(2,1)} custom-call(s32[4]{0:T(128)} %pad_add_fusion.where_ref, bf16[256,1024]{1,0:T(8,128)(2,1)} %bitcast.38, bf16[256,1024]{1,0:T(8,128)(2,1)} %copy-done.5, bf16[128,1024]{1,0:T(8,128)(2,1)} %copy-done.14, bf16[128,1024]{1,0:T(8,128)(2,1)} %copy-done.15, bf16[256,1024]{1,0:T(8,128)(2,1)} %copy-done.4, ...), custom_call_target="tpu_custom_call" | custom-call | tf_op jit(solution)/shard_map/project/pallas_call | solution.py:61
  182.3 7.9 %all-to-all-start = ((bf16[16,32,512]{2,1,0:T(8,128)(2,1)}), bf16[16,32,512]{2,1,0:T(8,128)(2,1)S(1)}, u32[]{:S(2)}, u32[]{:S(2)}) async-start(bf16[16,32,512]{2,1,0:T(8,128)(2,1)} %bitcast.34), calls=%async_computation | async-start | bytes 1048576 | tf_op jit(solution)/shard_map/all_to_all | solution.py:240
  190.9 1.3 pad_add_fusion.1.where_ref
  192.2 1.2 maximum_select_fusion.q_ref
  193.4 8.1 %all-to-all-done = bf16[16,32,512]{2,1,0:T(8,128)(2,1)S(1)} async-done(((bf16[16,32,512]{2,1,0:T(8,128)(2,1)}), bf16[16,32,512]{2,1,0:T(8,128)(2,1)S(1)}, u32[]{:S(2)}, u32[]{:S(2)}) %all-to-all-start) | async-done | bytes 524320 | tf_op jit(solution)/shard_map/all_to_all | solution.py:240
  202.3 10.5 %attend.1 = bf16[8,272,256]{2,1,0:T(8,128)(2,1)} custom-call(s32[2]{0:T(128)} %pad_add_fusion.1.where_ref, bf16[2048,256]{1,0:T(8,128)(2,1)} %maximum_select_fusion.q_ref, bf16[512,512]{1,0:T(8,128)(2,1)} %bitcast.43, bf16[512,512]{1,0:T(8,128)(2,1)} %bitcast.42), custom_call_target="tpu_custom_call" | custom-call | tf_op jit(solution)/shard_map/attend/pallas_call | solution.py:114
  212.8 2.0 dynamic-slice_bitcast_fusion
  214.8 2.2 collective-permute-start.19
  217.1 1.2 collective-permute-start.20
  218.2 3.6 %collective-permute-done.18.b_ref = bf16[2,272,256]{2,1,0:T(8,128)(2,1)S(1)} collective-permute-done((bf16[2,272,256]{2,1,0:T(8,128)(2,1)S(1)}, bf16[2,272,256]{2,1,0:T(8,128)(2,1)S(1)}, u32[]{:S(2)}, u32[]{:S(2)}) %collective-permute-start.18) | collective-permute-done | bytes 278560 | tf_op jit(solution)/shard_map/ppermute | solution.py:25
  222.6 7.1 %collective-permute-done.20.d_ref = bf16[2,272,256]{2,1,0:T(8,128)(2,1)S(1)} collective-permute-done((bf16[2,272,256]{2,1,0:T(8,128)(2,1)S(1)}, bf16[2,272,256]{2,1,0:T(8,128)(2,1)S(1)}, u32[]{:S(2)}, u32[]{:S(2)}) %collective-permute-start.20) | collective-permute-done | bytes 278560 | tf_op jit(solution)/shard_map/ppermute | solution.py:261
  230.4 2.2 merge.1
  232.6 1.0 broadcast_select_fusion.2
  233.6 2.2 collective-permute-start.21
  235.8 1.0 collective-permute-done.21
  237.0 2.5 collective-permute-start.23
  239.4 2.2 collective-permute-start.25
  243.6 5.2 %collective-permute-done.25.refs_4_ = bf16[64,512]{1,0:T(8,128)(2,1)S(1)} collective-permute-done((bf16[64,512]{1,0:T(8,128)(2,1)S(1)}, bf16[64,512]{1,0:T(8,128)(2,1)S(1)}, u32[]{:S(2)}, u32[]{:S(2)}) %collective-permute-start.25) | collective-permute-done | bytes 65568 | tf_op jit(solution)/shard_map/ppermute | solution.py:271
  248.8 1.4 collective-permute-start.26
  252.3 6.1 %output.1 = (f32[64,2048]{1,0:T(8,128)}, f32[64,2048]{1,0:T(8,128)}) custom-call(s32[4]{0:T(128)} %pad_add_fusion.where_ref, bf16[64,512]{1,0:T(8,128)(2,1)} %copy-done.13, bf16[64,512]{1,0:T(8,128)(2,1)} %copy-done.20, bf16[64,512]{1,0:T(8,128)(2,1)} %copy-done.17, bf16[64,512]{1,0:T(8,128)(2,1)} %copy-done.21, bf16[64,512]{1,0:T(8,128)(2,1)} %copy-done.18, ...), custom_call_target="tpu_custom_call" | custom-call | tf_op jit(solution)/shard_map/output/pallas_call | solution.py:170
  258.7 1.8 collective-permute-done.29.other
  261.3 2.5 finish.1
  (100 shorter events, 14.6 us)
Async XLA Ops:
  7.2 69.0 %copy-start.8 = (bf16[8,64,1024]{2,1,0:T(8,128)(2,1)S(1)}, bf16[8,64,1024]{2,1,0:T(8,128)(2,1)}, u32[]{:S(2)}) copy-start(bf16[8,64,1024]{2,1,0:T(8,128)(2,1)} %param.7) | copy-start | bytes 3145732
  7.2 68.0 %all-gather.3.cloned.1.call-start = ((), (), s32[]{:S(2)}) async-start(), calls=%async_computation.2 | async-start | bytes 4456448 | tf_op jit(solution)/shard_map/all_gather | solution.py:216
  8.2 4.7 %collective-permute-start.7 = (bf16[64,512]{1,0:T(8,128)(2,1)S(1)}, bf16[64,512]{1,0:T(8,128)(2,1)S(1)}, u32[]{:S(2)}, u32[]{:S(2)}) collective-permute-start(bf16[64,512]{1,0:T(8,128)(2,1)S(1)} %get-tuple-element.25), channel_id=1, source_target_pairs={{0,1},{1,0},{2,3},{3,2},{4,5},{5,4},{6,7},{7,6},{8,9},{9,8},{10,11... | collective-permute-start | bytes 196616 | tf_op jit(solution)/shard_map/ppermute | solution.py:25
  11.5 4.9 %collective-permute-start.9 = (bf16[64,512]{1,0:T(8,128)(2,1)S(1)}, bf16[64,512]{1,0:T(8,128)(2,1)S(1)}, u32[]{:S(2)}, u32[]{:S(2)}) collective-permute-start(bf16[64,512]{1,0:T(8,128)(2,1)S(1)} %get-tuple-element.25), channel_id=1, source_target_pairs={{0,3},{1,2},{2,1},{3,0},{4,7},{5,6},{6,5},{7,4},{8,11},{9,10},{10,... | collective-permute-start | bytes 196616 | tf_op jit(solution)/shard_map/ppermute | solution.py:214
  11.5 4.9 %collective-permute-start.8 = (bf16[64,512]{1,0:T(8,128)(2,1)S(1)}, bf16[64,512]{1,0:T(8,128)(2,1)S(1)}, u32[]{:S(2)}, u32[]{:S(2)}) collective-permute-start(bf16[64,512]{1,0:T(8,128)(2,1)S(1)} %get-tuple-element.24), channel_id=1, source_target_pairs={{0,2},{2,0},{1,3},{3,1},{4,6},{6,4},{5,7},{7,5},{8,10},{10,8},{9,1... | collective-permute-start | bytes 196616 | tf_op jit(solution)/shard_map/ppermute | solution.py:25
  17.2 234.4 %all-gather.5.cloned.1.call-start = ((), (), s32[]{:S(2)}) async-start(), calls=%async_computation.3 | async-start | bytes 8912896 | tf_op jit(solution)/shard_map/all_gather | solution.py:234
  18.2 86.4 %copy-start.16 = (bf16[256,512]{1,0:T(8,128)(2,1)S(1)}, bf16[256,512]{1,0:T(8,128)(2,1)}, u32[]{:S(2)}) copy-start(bf16[256,512]{1,0:T(8,128)(2,1)} %param.10) | copy-start | bytes 786436
  18.2 8.9 %collective-permute-start.10 = (bf16[512,128]{1,0:T(8,128)(2,1)S(1)}, bf16[512,128]{1,0:T(8,128)(2,1)S(1)}, u32[]{:S(2)}, u32[]{:S(2)}) collective-permute-start(bf16[512,128]{1,0:T(8,128)(2,1)S(1)} %constant_dynamic-slice_fusion), channel_id=1, source_target_pairs={{0,192},{64,0},{128,64},{192,128},{1,193},{65,1},{129,65},{193,129... | collective-permute-start | bytes 393224 | tf_op jit(solution)/shard_map/ppermute | solution.py:230
  22.6 10.9 %collective-permute-start.11 = (bf16[512,128]{1,0:T(8,128)(2,1)S(1)}, bf16[512,128]{1,0:T(8,128)(2,1)S(1)}, u32[]{:S(2)}, u32[]{:S(2)}) collective-permute-start(bf16[512,128]{1,0:T(8,128)(2,1)S(1)} %constant_dynamic-slice_fusion), channel_id=1, source_target_pairs={{0,128},{64,192},{128,0},{192,64},{1,129},{65,193},{129,1},{193,65... | collective-permute-start | bytes 393224 | tf_op jit(solution)/shard_map/ppermute | solution.py:230
  23.6 10.0 %collective-permute-start.12 = (bf16[512,128]{1,0:T(8,128)(2,1)S(1)}, bf16[512,128]{1,0:T(8,128)(2,1)S(1)}, u32[]{:S(2)}, u32[]{:S(2)}) collective-permute-start(bf16[512,128]{1,0:T(8,128)(2,1)S(1)} %constant_dynamic-slice_fusion), channel_id=1, source_target_pairs={{0,64},{64,128},{128,192},{192,0},{1,65},{65,129},{129,193},{193,1... | collective-permute-start | bytes 393224 | tf_op jit(solution)/shard_map/ppermute | solution.py:230
  75.2 71.4 %collective-permute-start.13 = (bf16[4096,512]{1,0:T(8,128)(2,1)}, bf16[4096,512]{1,0:T(8,128)(2,1)}, u32[]{:S(2)}, u32[]{:S(2)}) collective-permute-start(bf16[4096,512]{1,0:T(8,128)(2,1)} %all-gather.3.cloned.1.call-done.w_mine), channel_id=1, source_target_pairs={{0,1},{1,0},{2,3},{3,2},{4,5},{5,4},{6,7},{7,6},{8,9},{9,8},{10,11... | collective-permute-start | bytes 12582920 | tf_op jit(solution)/shard_map/ppermute | solution.py:25
  76.2 70.3 %copy-start.1 = (bf16[8,32,1024]{2,1,0:T(8,128)(2,1)}, bf16[8,32,1024]{2,1,0:T(8,128)(2,1)S(1)}, u32[]{:S(2)}) copy-start(bf16[8,32,1024]{2,1,0:T(8,128)(2,1)S(1)} %get-tuple-element.14) | copy-start | bytes 1572868
  76.3 77.6 %copy-start = (bf16[8,32,1024]{2,1,0:T(8,128)(2,1)}, bf16[8,32,1024]{2,1,0:T(8,128)(2,1)S(1)}, u32[]{:S(2)}) copy-start(bf16[8,32,1024]{2,1,0:T(8,128)(2,1)S(1)} %get-tuple-element.15) | copy-start | bytes 1572868
  76.3 23.5 %collective-permute-start.15 = (bf16[256,1024]{1,0:T(8,128)(2,1)S(1)}, bf16[256,1024]{1,0:T(8,128)(2,1)S(1)}, u32[]{:S(2)}, u32[]{:S(2)}) collective-permute-start(bf16[256,1024]{1,0:T(8,128)(2,1)S(1)} %bitcast.39), channel_id=1, source_target_pairs={{0,64},{64,128},{128,192},{192,0},{1,65},{65,129},{129,193},{193,1... | collective-permute-start | bytes 1572872 | tf_op jit(solution)/shard_map/ppermute | solution.py:223
  78.6 31.6 %collective-permute-start.14 = (bf16[256,1024]{1,0:T(8,128)(2,1)S(1)}, bf16[256,1024]{1,0:T(8,128)(2,1)S(1)}, u32[]{:S(2)}, u32[]{:S(2)}) collective-permute-start(bf16[256,1024]{1,0:T(8,128)(2,1)S(1)} %bitcast.40), channel_id=1, source_target_pairs={{0,192},{64,0},{128,64},{192,128},{1,193},{65,1},{129,65},{193,129... | collective-permute-start | bytes 1572872 | tf_op jit(solution)/shard_map/ppermute | solution.py:224
  99.8 46.8 %copy-start.6 = (bf16[256,1024]{1,0:T(8,128)(2,1)}, bf16[256,1024]{1,0:T(8,128)(2,1)S(1)}, u32[]{:S(2)}) copy-start(bf16[256,1024]{1,0:T(8,128)(2,1)S(1)} %collective-permute-done.15.prev) | copy-start | bytes 1572868
  99.8 15.8 %collective-permute-start.16 = (bf16[128,1024]{1,0:T(8,128)(2,1)S(1)}, bf16[128,1024]{1,0:T(8,128)(2,1)}, u32[]{:S(2)}, u32[]{:S(2)}) collective-permute-start(bf16[128,1024]{1,0:T(8,128)(2,1)S(1)} %slice.56), channel_id=1, source_target_pairs={{0,64},{64,128},{128,192},{192,0},{1,65},{65,129},{129,193},{193,1... | collective-permute-start | bytes 786440 | tf_op jit(solution)/shard_map/ppermute | solution.py:225
  104.6 6.4 %collective-permute-start = (bf16[256,256]{1,0:T(8,128)(2,1)S(1)}, bf16[256,256]{1,0:T(8,128)(2,1)S(1)}, u32[]{:S(2)}, u32[]{:S(2)}) collective-permute-start(bf16[256,256]{1,0:T(8,128)(2,1)S(1)} %get-tuple-element.23), channel_id=1, source_target_pairs={{0,1},{1,0},{2,3},{3,2},{4,5},{5,4},{6,7},{7,6},{8,9},{9,8},{10,11... | collective-permute-start | bytes 393224 | tf_op jit(solution)/shard_map/ppermute | solution.py:25
  105.9 55.2 %collective-permute-start.4 = (bf16[256,1024]{1,0:T(8,128)(2,1)S(1)}, bf16[256,1024]{1,0:T(8,128)(2,1)S(1)}, u32[]{:S(2)}, u32[]{:S(2)}) collective-permute-start(bf16[256,1024]{1,0:T(8,128)(2,1)S(1)} %bitcast.36), channel_id=1, source_target_pairs={{0,64},{64,128},{128,192},{192,0},{1,65},{65,129},{129,193},{193,1... | collective-permute-start | bytes 1572872 | tf_op jit(solution)/shard_map/ppermute | solution.py:223
  110.2 36.4 %copy-start.7 = (bf16[256,1024]{1,0:T(8,128)(2,1)}, bf16[256,1024]{1,0:T(8,128)(2,1)S(1)}, u32[]{:S(2)}) copy-start(bf16[256,1024]{1,0:T(8,128)(2,1)S(1)} %collective-permute-done.14.nxt) | copy-start | bytes 1572868
  110.2 53.0 %collective-permute-start.3 = (bf16[256,1024]{1,0:T(8,128)(2,1)S(1)}, bf16[256,1024]{1,0:T(8,128)(2,1)S(1)}, u32[]{:S(2)}, u32[]{:S(2)}) collective-permute-start(bf16[256,1024]{1,0:T(8,128)(2,1)S(1)} %bitcast.37), channel_id=1, source_target_pairs={{0,192},{64,0},{128,64},{192,128},{1,193},{65,1},{129,65},{193,129... | collective-permute-start | bytes 1572872 | tf_op jit(solution)/shard_map/ppermute | solution.py:224
  111.0 35.6 %collective-permute-start.17 = (bf16[128,1024]{1,0:T(8,128)(2,1)}, bf16[128,1024]{1,0:T(8,128)(2,1)}, u32[]{:S(2)}, u32[]{:S(2)}) collective-permute-start(bf16[128,1024]{1,0:T(8,128)(2,1)} %slice.57), channel_id=1, source_target_pairs={{0,192},{64,0},{128,64},{192,128},{1,193},{65,1},{129,65},{193,129... | collective-permute-start | bytes 786440 | tf_op jit(solution)/shard_map/ppermute | solution.py:226
  115.6 44.1 %collective-permute-start.1 = (bf16[512,256]{1,0:T(8,128)(2,1)S(1)}, bf16[512,256]{1,0:T(8,128)(2,1)}, u32[]{:S(2)}, u32[]{:S(2)}) collective-permute-start(bf16[512,256]{1,0:T(8,128)(2,1)S(1)} %maximum_select_fusion.2), channel_id=1, source_target_pairs={{0,2},{2,0},{1,3},{3,1},{4,6},{6,4},{5,7},{7,5},{8,10},{10,8},{9,1... | collective-permute-start | bytes 786440 | tf_op jit(solution)/shard_map/ppermute | solution.py:25
  153.9 28.4 %all-to-all-start.1 = ((bf16[16,32,512]{2,1,0:T(8,128)(2,1)}), bf16[16,32,512]{2,1,0:T(8,128)(2,1)S(1)}, u32[]{:S(2)}, u32[]{:S(2)}) async-start(bf16[16,32,512]{2,1,0:T(8,128)(2,1)} %bitcast.35), calls=%async_computation.1 | async-start | bytes 1048576 | tf_op jit(solution)/shard_map/all_to_all | solution.py:240
  160.9 31.3 %collective-permute-start.2 = (bf16[1024,256]{1,0:T(8,128)(2,1)S(1)}, bf16[1024,256]{1,0:T(8,128)(2,1)S(1)}, u32[]{:S(2)}, u32[]{:S(2)}) collective-permute-start(bf16[1024,256]{1,0:T(8,128)(2,1)S(1)} %maximum_select_fusion.1), channel_id=1, source_target_pairs={{0,4},{4,0},{1,5},{5,1},{2,6},{6,2},{3,7},{7,3},{8,12},{12,8},{9,1... | collective-permute-start | bytes 1572872 | tf_op jit(solution)/shard_map/ppermute | solution.py:25
  161.1 13.5 %copy-start.4 = (bf16[256,1024]{1,0:T(8,128)(2,1)}, bf16[256,1024]{1,0:T(8,128)(2,1)S(1)}, u32[]{:S(2)}) copy-start(bf16[256,1024]{1,0:T(8,128)(2,1)S(1)} %collective-permute-done.4.prev) | copy-start | bytes 1572868
  161.1 9.7 %collective-permute-start.5 = (bf16[128,1024]{1,0:T(8,128)(2,1)S(1)}, bf16[128,1024]{1,0:T(8,128)(2,1)S(1)}, u32[]{:S(2)}, u32[]{:S(2)}) collective-permute-start(bf16[128,1024]{1,0:T(8,128)(2,1)S(1)} %slice.54), channel_id=1, source_target_pairs={{0,64},{64,128},{128,192},{192,0},{1,65},{65,129},{129,193},{193,1... | collective-permute-start | bytes 786440 | tf_op jit(solution)/shard_map/ppermute | solution.py:225
  163.2 11.4 %copy-start.5 = (bf16[256,1024]{1,0:T(8,128)(2,1)}, bf16[256,1024]{1,0:T(8,128)(2,1)S(1)}, u32[]{:S(2)}) copy-start(bf16[256,1024]{1,0:T(8,128)(2,1)S(1)} %collective-permute-done.3.nxt) | copy-start | bytes 1572868
  163.2 27.0 %copy-start.24 = (s32[8]{0:T(128)S(1)}, s32[8]{0:T(128)}, u32[]{:S(2)}) copy-start(s32[8]{0:T(128)} %param.9) | copy-start | bytes 100
  163.3 11.3 %collective-permute-start.6 = (bf16[128,1024]{1,0:T(8,128)(2,1)S(1)}, bf16[128,1024]{1,0:T(8,128)(2,1)S(1)}, u32[]{:S(2)}, u32[]{:S(2)}) collective-permute-start(bf16[128,1024]{1,0:T(8,128)(2,1)S(1)} %slice.55), channel_id=1, source_target_pairs={{0,192},{64,0},{128,64},{192,128},{1,193},{65,1},{129,65},{193,129... | collective-permute-start | bytes 786440 | tf_op jit(solution)/shard_map/ppermute | solution.py:226
  182.3 19.2 %copy-start.2 = (bf16[16,32,512]{2,1,0:T(8,128)(2,1)}, bf16[16,32,512]{2,1,0:T(8,128)(2,1)S(1)}, u32[]{:S(2)}) copy-start(bf16[16,32,512]{2,1,0:T(8,128)(2,1)S(1)} %all-to-all-done.1) | copy-start | bytes 1572868
  182.3 19.1 %all-to-all-start = ((bf16[16,32,512]{2,1,0:T(8,128)(2,1)}), bf16[16,32,512]{2,1,0:T(8,128)(2,1)S(1)}, u32[]{:S(2)}, u32[]{:S(2)}) async-start(bf16[16,32,512]{2,1,0:T(8,128)(2,1)} %bitcast.34), calls=%async_computation | async-start | bytes 1048576 | tf_op jit(solution)/shard_map/all_to_all | solution.py:240
  214.8 7.0 %collective-permute-start.18 = (bf16[2,272,256]{2,1,0:T(8,128)(2,1)S(1)}, bf16[2,272,256]{2,1,0:T(8,128)(2,1)S(1)}, u32[]{:S(2)}, u32[]{:S(2)}) collective-permute-start(bf16[2,272,256]{2,1,0:T(8,128)(2,1)S(1)} %get-tuple-element.12), channel_id=1, source_target_pairs={{0,4},{4,0},{1,5},{5,1},{2,6},{6,2},{3,7},{7,3},{8,12},{12,8},{9,1... | collective-permute-start | bytes 835592 | tf_op jit(solution)/shard_map/ppermute | solution.py:25
  214.8 7.8 %collective-permute-start.19 = (bf16[2,272,256]{2,1,0:T(8,128)(2,1)S(1)}, bf16[2,272,256]{2,1,0:T(8,128)(2,1)S(1)}, u32[]{:S(2)}, u32[]{:S(2)}) collective-permute-start(bf16[2,272,256]{2,1,0:T(8,128)(2,1)S(1)} %get-tuple-element.11), channel_id=1, source_target_pairs={{0,2},{2,0},{1,3},{3,1},{4,6},{6,4},{5,7},{7,5},{8,10},{10,8},{9,1... | collective-permute-start | bytes 835592 | tf_op jit(solution)/shard_map/ppermute | solution.py:25
  217.1 12.7 %collective-permute-start.20 = (bf16[2,272,256]{2,1,0:T(8,128)(2,1)S(1)}, bf16[2,272,256]{2,1,0:T(8,128)(2,1)S(1)}, u32[]{:S(2)}, u32[]{:S(2)}) collective-permute-start(bf16[2,272,256]{2,1,0:T(8,128)(2,1)S(1)} %get-tuple-element.10), channel_id=1, source_target_pairs={{0,6},{2,4},{4,2},{6,0},{1,7},{3,5},{5,3},{7,1},{8,14},{10,12},{12... | collective-permute-start | bytes 835592 | tf_op jit(solution)/shard_map/ppermute | solution.py:261
  221.8 7.9 %copy-start.10 = (bf16[2,272,256]{2,1,0:T(8,128)(2,1)}, bf16[2,272,256]{2,1,0:T(8,128)(2,1)S(1)}, u32[]{:S(2)}) copy-start(bf16[2,272,256]{2,1,0:T(8,128)(2,1)S(1)} %collective-permute-done.18.b_ref) | copy-start | bytes 835588
  222.6 7.1 %copy-start.11 = (bf16[2,272,256]{2,1,0:T(8,128)(2,1)}, bf16[2,272,256]{2,1,0:T(8,128)(2,1)S(1)}, u32[]{:S(2)}) copy-start(bf16[2,272,256]{2,1,0:T(8,128)(2,1)S(1)} %collective-permute-done.19.c_ref) | copy-start | bytes 835588
  233.6 3.2 %collective-permute-start.21 = (bf16[256,256]{1,0:T(8,128)(2,1)S(1)}, bf16[256,256]{1,0:T(8,128)(2,1)S(1)}, u32[]{:S(2)}, u32[]{:S(2)}) collective-permute-start(bf16[256,256]{1,0:T(8,128)(2,1)S(1)} %get-tuple-element.21), channel_id=1, source_target_pairs={{0,1},{1,0},{2,3},{3,2},{4,5},{5,4},{6,7},{7,6},{8,9},{9,8},{10,11... | collective-permute-start | bytes 393224 | tf_op jit(solution)/shard_map/ppermute | solution.py:25
  236.9 14.7 %copy-start.13 = (bf16[64,512]{1,0:T(8,128)(2,1)}, bf16[64,512]{1,0:T(8,128)(2,1)S(1)}, u32[]{:S(2)}) copy-start(bf16[64,512]{1,0:T(8,128)(2,1)S(1)} %get-tuple-element.19.refs_0_) | copy-start | bytes 196612
  237.0 5.8 %collective-permute-start.23 = (bf16[64,512]{1,0:T(8,128)(2,1)S(1)}, bf16[64,512]{1,0:T(8,128)(2,1)S(1)}, u32[]{:S(2)}, u32[]{:S(2)}) collective-permute-start(bf16[64,512]{1,0:T(8,128)(2,1)S(1)} %get-tuple-element.18), channel_id=1, source_target_pairs={{0,192},{64,0},{128,64},{192,128},{1,193},{65,1},{129,65},{193,129... | collective-permute-start | bytes 196616 | tf_op jit(solution)/shard_map/ppermute | solution.py:271
  239.4 9.3 %collective-permute-start.25 = (bf16[64,512]{1,0:T(8,128)(2,1)S(1)}, bf16[64,512]{1,0:T(8,128)(2,1)S(1)}, u32[]{:S(2)}, u32[]{:S(2)}) collective-permute-start(bf16[64,512]{1,0:T(8,128)(2,1)S(1)} %get-tuple-element.17), channel_id=1, source_target_pairs={{0,128},{64,192},{128,0},{192,64},{1,129},{65,193},{129,1},{193,65... | collective-permute-start | bytes 196616 | tf_op jit(solution)/shard_map/ppermute | solution.py:271
  241.6 8.6 %collective-permute-start.27 = (bf16[64,512]{1,0:T(8,128)(2,1)S(1)}, bf16[64,512]{1,0:T(8,128)(2,1)S(1)}, u32[]{:S(2)}, u32[]{:S(2)}) collective-permute-start(bf16[64,512]{1,0:T(8,128)(2,1)S(1)} %get-tuple-element.16), channel_id=1, source_target_pairs={{0,64},{64,128},{128,192},{192,0},{1,65},{65,129},{129,193},{193,1... | collective-permute-start | bytes 196616 | tf_op jit(solution)/shard_map/ppermute | solution.py:271
  241.8 8.9 %collective-permute-start.22 = (bf16[64,512]{1,0:T(8,128)(2,1)S(1)}, bf16[64,512]{1,0:T(8,128)(2,1)S(1)}, u32[]{:S(2)}, u32[]{:S(2)}) collective-permute-start(bf16[64,512]{1,0:T(8,128)(2,1)S(1)} %get-tuple-element.19.refs_0_), channel_id=1, source_target_pairs={{0,1},{1,0},{2,3},{3,2},{4,5},{5,4},{6,7},{7,6},{8,9},{9,8},{10,11... | collective-permute-start | bytes 196616 | tf_op jit(solution)/shard_map/ppermute | solution.py:25
  242.8 8.9 %copy-start.17 = (bf16[64,512]{1,0:T(8,128)(2,1)}, bf16[64,512]{1,0:T(8,128)(2,1)S(1)}, u32[]{:S(2)}) copy-start(bf16[64,512]{1,0:T(8,128)(2,1)S(1)} %collective-permute-done.23.refs_2_) | copy-start | bytes 196612
  242.8 8.0 %collective-permute-start.24 = (bf16[64,512]{1,0:T(8,128)(2,1)S(1)}, bf16[64,512]{1,0:T(8,128)(2,1)S(1)}, u32[]{:S(2)}, u32[]{:S(2)}) collective-permute-start(bf16[64,512]{1,0:T(8,128)(2,1)S(1)} %collective-permute-done.23.refs_2_), channel_id=1, source_target_pairs={{0,1},{1,0},{2,3},{3,2},{4,5},{5,4},{6,7},{7,6},{8,9},{9,8},{10,11... | collective-permute-start | bytes 196616 | tf_op jit(solution)/shard_map/ppermute | solution.py:25
  248.8 2.3 collective-permute-start.26
  250.2 1.4 collective-permute-start.28
  258.4 2.1 collective-permute-start.29
  (11 other events, 14.3 us)
Sparse Core Ops, SparseCore 0:
  17.3 57.8 all-gather.2
  77.6 80.7 all-gather.4
where the time goes:
time: 271 us
  waiting for transfers between devices  143 us (53%)
  starting transfers between devices  61.7 us (23%)
  Pallas kernels  35.7 us (13%)
  between operations  14.3 us (5%)
  other arithmetic  8.2 us (3%)
  local copies, waits for them, and re-layouts  8.11 us (3%)
    all_gather x1, waiting for transfers between devices, shards(): w_mine = lax.all_gather(rows, XY, axis=0, tiled=True)  40.8 us
    ppermute x2, waiting for transfers between devices, shards(): opp_b = lax.ppermute(nxt[half:], Z, BWD)  32.4 us
    ppermute x2, waiting for transfers between devices, shards(): prev = lax.ppermute(own, Z, FWD)  19.5 us
    ppermute x14, starting transfers between devices, swap(): return lax.ppermute(a, axis, [(0, 1), (1, 0)])  17.4 us
    pallas_call x2, Pallas kernels, project(): pl.pallas_call(project_kernel, out_shape=jax.ShapeDtypeStruct((8, 2, rows...  14.3 us
    all_to_all x2, starting transfers between devices, shards(): lax.all_to_all(both.reshape(16, step, 512), (X, 'yh', 'c'), 0, 0, tiled=T...  13.7 us
    ppermute x14, waiting for transfers between devices, swap(): return lax.ppermute(a, axis, [(0, 1), (1, 0)])  11.4 us
    pallas_call x1, Pallas kernels, attend(): pl.pallas_call(functools.partial(attend_kernel, rows), grid=(tokens // 25...  10.5 us
  transfers between devices with their start and end apart: 34, of which 18 were waited for; matrix products, arithmetic and copies ran while one was open for 4% of the time, Pallas kernels for 10%

commit v1 on v0

v1 whole, which is shorter than its diff:
```python
import functools
import math

import jax
import jax.numpy as jnp
from jax import lax
from jax.experimental import pallas as pl
from jax.experimental.pallas import tpu as pltpu
from jax.sharding import Mesh, PartitionSpec as P


DH = 256
CHUNKS = 2
BF = jnp.bfloat16
F32 = jnp.float32
X = "x"
XY = ("x", "yh", "yl")
Z = "zh"
EXP_SCALE = math.log2(math.e) / math.sqrt(DH)
FWD = [(i, (i + 1) % 4) for i in range(4)]
BWD = [(i, (i + 3) % 4) for i in range(4)]


def swap(a, axis):
    return lax.ppermute(a, axis, [(0, 1), (1, 0)])


def pair(a, b, index, axis=0):
    return jnp.where(index == 0, jnp.concatenate([a, b], axis), jnp.concatenate([b, a], axis))


def pick(a, b, index):
    return jnp.where(index == 0, a, b)


def project_kernel(where_ref, own, nxt, opp_a, opp_b, prev, w_mine, w_theirs, out_ref, buf, sem):
    zh, c = where_ref[0], where_ref[3]
    copies = []
    for dz in range(4):
        block = pl.ds(pl.multiple_of(lax.rem(zh + dz, 4) * 1024, 1024), 1024)
        for j, w in enumerate((w_mine, w_theirs)):
            copies.append(pltpu.make_async_copy(w.at[block], buf.at[2 * dz + j], sem.at[2 * dz + j]))
            copies[-1].start()
    acc = [jnp.zeros((own.shape[0], 2 * DH), F32)] * 2
    for dz in range(4):
        if dz == 2:
            rows = jnp.concatenate([opp_a[...], opp_b[...]], 0)
        else:
            rows = (own, nxt, None, prev)[dz][...]
        for j in range(2):
            copies[2 * dz + j].wait()
            acc[j] = acc[j] + jnp.dot(rows, buf[2 * dz + j], preferred_element_type=F32)
    shape = (out_ref.shape[0],) + out_ref.shape[2:]
    out_ref[:, c] = acc[0].astype(BF).reshape(shape)
    out_ref[:, 1 - c] = acc[1].astype(BF).reshape(shape)


def project(where, pieces, weights):
    rows = pieces[0].shape[0]
    vmem = pl.BlockSpec(memory_space=pltpu.VMEM)
    return pl.pallas_call(
        project_kernel,
        out_shape=jax.ShapeDtypeStruct((8, 2, rows // 8, 2 * DH), BF),
        in_specs=[pl.BlockSpec(memory_space=pltpu.SMEM)] + [vmem] * 5 + [pl.BlockSpec(memory_space=pl.ANY)] * 2,
        out_specs=vmem,
        scratch_shapes=[pltpu.VMEM((8, 1024, 2 * DH), BF), pltpu.SemaphoreType.DMA((8,))],
        name="project",
    )(where, *pieces, *weights)


def attend_kernel(chunk, last, where_ref, q_ref, kv_ref, *refs):
    length, base = where_ref[0], where_ref[1]
    step = pl.program_id(0)
    rows = kv_ref.shape[0]
    per = rows // 16
    bias_ref, vt_ref = refs[-2:]
    if last:
        acc_in, stats_in, outs = refs[0], refs[1], refs[2:6]
    else:
        acc_out, stats_out = refs[0], refs[1]

    @pl.when(step == 0)
    def _():
        row = lax.broadcasted_iota(jnp.int32, (rows, 128), 0)
        source = row // (2 * per)
        side = (row // per) % 2
        position = source * 512 + base + side * 64 + chunk * per + row % per
        bias_ref[...] = jnp.where(position < length, 0.0, -1e30)
        vt_ref[...] = kv_ref[:, DH:].T

    q = q_ref[...]
    s = lax.dot_general(kv_ref[:, :DH], q, (((1,), (1,)), ((), ())), preferred_element_type=F32)
    bias = bias_ref[...]
    s = s + jnp.concatenate([bias, bias], axis=1)
    high = jnp.max(s, axis=0, keepdims=True)
    if last:
        before = stats_in[0, 0:1]
        high = jnp.maximum(high, before)
    p = jnp.exp2((s - high) * EXP_SCALE)
    total = jnp.sum(p, axis=0, keepdims=True)
    acc = jnp.dot(vt_ref[...], p.astype(BF), preferred_element_type=F32)
    if not last:
        acc_out[0] = acc
        stats_out[0] = jnp.concatenate([high, total, jnp.zeros((6, 256), F32)], 0)
        return
    keep = jnp.exp2((before - high) * EXP_SCALE)
    total = total + stats_in[0, 1:2] * keep
    acc = acc + acc_in[0] * keep
    context = (acc * (1.0 / total)).astype(BF)
    lse = high * EXP_SCALE + jnp.log2(total)
    first = lse.astype(BF).astype(F32)
    second = (lse - first).astype(BF).astype(F32)
    third = lse - first - second
    stats = jnp.concatenate([first, second, third, jnp.zeros((13, 256), F32)], 0).astype(BF)
    for r, out in enumerate(outs):

        @pl.when(step // 2 == r)
        def _(out=out):
            out[0, :DH] = context
            out[0, DH:] = stats


def attend(where, q, kv, chunk, before=None):
    last = before is not None
    rows = kv.shape[0]

    def block(i, where):
        return where[2 + i // 2] * 2 + i % 2

    state = [pl.BlockSpec((1, DH, 256), lambda i, w: (i, 0, 0)), pl.BlockSpec((1, 8, 256), lambda i, w: (i, 0, 0))]
    if last:
        outs = [jax.ShapeDtypeStruct((2, DH + 16, 256), BF)] * 4
        out_specs = [
            pl.BlockSpec((1, DH + 16, 256), lambda i, w, r=r: (jnp.clip(i - 2 * r, 0, 1), 0, 0)) for r in range(4)
        ]
    else:
        outs = [jax.ShapeDtypeStruct((8, DH, 256), F32), jax.ShapeDtypeStruct((8, 8, 256), F32)]
        out_specs = state
    return pl.pallas_call(
        functools.partial(attend_kernel, chunk, last),
        out_shape=outs,
        grid_spec=pltpu.PrefetchScalarGridSpec(
            num_scalar_prefetch=1,
            grid=(8,),
            in_specs=[
                pl.BlockSpec((256, DH), lambda i, w: (block(i, w), 0)),
                pl.BlockSpec((rows, 2 * DH), lambda i, w: (0, 0)),
            ]
            + (state if last else []),
            out_specs=out_specs,
            scratch_shapes=[pltpu.VMEM((rows, 128), F32), pltpu.VMEM((DH, rows), BF)],
        ),
        name="attend",
    )(where, q, kv, *(before or ()))


def merge_kernel(where_ref, a_ref, b_ref, c_ref, d_ref, *outs):
    zh = where_ref[0]
    refs = (a_ref, b_ref, c_ref, d_ref)
    contexts = []
    for side in range(2):
        stats = [ref[side, DH:].astype(F32) for ref in refs]
        lse = [s[0:1] + s[1:2] + s[2:3] for s in stats]
        high = functools.reduce(jnp.maximum, lse)
        weight = [jnp.exp2(v - high) for v in lse]
        inverse = 1.0 / sum(weight)
        context = sum(ref[side, :DH].astype(F32) * (w * inverse) for ref, w in zip(refs, weight))
        contexts.append(context.T.astype(BF))
    for d in range(4):
        for m in range(4):

            @pl.when(lax.rem(zh + d, 4) == m)
            def _(d=d, m=m):
                for side in range(2):
                    outs[d][side * 64 : (side + 1) * 64] = contexts[side][m * 64 : (m + 1) * 64]


def merge(where, parts):
    vmem = pl.BlockSpec(memory_space=pltpu.VMEM)
    return pl.pallas_call(
        merge_kernel,
        out_shape=[jax.ShapeDtypeStruct((128, DH), BF)] * 4,
        in_specs=[pl.BlockSpec(memory_space=pltpu.SMEM)] + [vmem] * 4,
        out_specs=[vmem] * 4,
        name="merge",
    )(where, *parts)


def output_kernel(where_ref, *refs):
    c = where_ref[3]
    w_ref, out_mine, out_theirs = refs[4:]
    rows = jnp.concatenate([ref[...] for ref in refs[:4]], 1)
    acc = jnp.dot(rows, w_ref[...], preferred_element_type=F32)
    low, high = acc[:64], acc[64:]
    out_mine[...] = jnp.where(c == 0, low, high)
    out_theirs[...] = jnp.where(c == 0, high, low)


def output(where, ctx, w):
    whole = pl.BlockSpec((128, DH), lambda i: (0, 0))
    out = pl.BlockSpec((64, 512), lambda i: (0, i))
    return pl.pallas_call(
        output_kernel,
        grid=(8,),
        out_shape=[jax.ShapeDtypeStruct((64, 4096), F32)] * 2,
        in_specs=[pl.BlockSpec(memory_space=pltpu.SMEM)] + [whole] * 4 + [pl.BlockSpec((1024, 512), lambda i: (0, i))],
        out_specs=[out] * 2,
        name="output",
    )(where, *ctx, w)


def finish_kernel(mine, other, residual, gain, hidden, normed):
    x = residual[...].astype(F32) + (mine[...] + other[...])
    scale = lax.rsqrt(jnp.mean(x * x, -1, keepdims=True) + 1e-06)
    hidden[...] = x.astype(BF)
    normed[...] = (x * scale * gain[...]).astype(BF)


def finish(mine, other, residual, gain):
    rows = pl.BlockSpec((16, 4096), lambda i: (i, 0))
    return pl.pallas_call(
        finish_kernel,
        grid=(4,),
        out_shape=[jax.ShapeDtypeStruct(residual.shape, BF)] * 2,
        in_specs=[rows] * 3 + [pl.BlockSpec((1, 4096), lambda i: (0, 0))],
        out_specs=[rows] * 2,
        name="finish",
    )(mine, other, residual, gain)


def shards(memory, kv_weight, mem_lengths, queries, out_weight, residual, norm_gain):
    zh, x, yh, yl, zl, c = (lax.axis_index(a) for a in (Z, X, "yh", "yl", "zl", "c"))
    y = yh * 2 + yl
    where = jnp.stack([zh, x, y, c]).astype(jnp.int32)

    mine = pick(kv_weight[:, :512], kv_weight[:, 512:], c)
    theirs = pick(kv_weight[:, 512:], kv_weight[:, :512], c)
    w_c = swap(theirs, "c")
    w_z = swap(mine, "zl")
    w_zc = lax.ppermute(theirs, ("zl", "c"), [(i, 3 - i) for i in range(4)])
    rows = pair(pair(mine, w_c, c), pair(w_z, w_zc, c), zl)
    w_mine = lax.all_gather(rows, XY, axis=0, tiled=True)

    step = memory.shape[1] // CHUNKS
    half = 4 * step
    chunks = []
    for j in range(CHUNKS):
        own = memory[:, j * step : (j + 1) * step].reshape(8 * step, 1024)
        prev = lax.ppermute(own, Z, FWD)
        nxt = lax.ppermute(own, Z, BWD)
        opp_a = lax.ppermute(prev[:half], Z, FWD)
        opp_b = lax.ppermute(nxt[half:], Z, BWD)
        chunks.append([own, nxt, opp_a, opp_b, prev])

    ow = lax.dynamic_slice(out_weight, (c * DH, (x * 4 + y) * 256), (DH, 256))
    ow = [ow] + [lax.ppermute(ow, Z, [(i, (i + 4 - d) % 4) for i in range(4)]) for d in (1, 2, 3)]
    ow = jnp.concatenate(ow, 0)

    w_mine, ow = lax.optimization_barrier((w_mine, ow))
    ow = lax.all_gather(ow, XY, axis=1, tiled=True)
    w_theirs = swap(w_mine, "c")

    other = pick(queries[:, DH:], queries[:, :DH], c)
    other = swap(other, "c")
    q = pair(pick(queries[:, :DH], queries[:, DH:], c), other, c)
    q = pair(q, swap(q, "zl"), zl)
    q = pair(q, swap(q, "yl"), yl)

    length = lax.dynamic_index_in_dim(mem_lengths, x * 2 + yh, 0, keepdims=False)
    here = yl * 2 + zl
    here = jnp.stack([length, yl * 256 + zl * 128, here, here ^ 1, here ^ 2, here ^ 3]).astype(jnp.int32)
    state = None
    for j, pieces in enumerate(chunks):
        both = project(where, pieces, (w_mine, w_theirs))
        both = lax.all_to_all(both.reshape(16, step, 512), (X, "yh", "c"), 0, 0, tiled=True)
        state = attend(here, q, both.reshape(16 * step, 512), j, state)

    own, to_zl, to_yl, to_both = state
    parts = (
        own,
        swap(to_zl, "zl"),
        swap(to_yl, "yl"),
        lax.ppermute(to_both, ("yl", "zl"), [(i, 3 - i) for i in range(4)]),
    )
    pieces = merge(where, parts)
    ctx = [pieces[0]] + [lax.ppermute(pieces[4 - d], Z, [(i, (i + 4 - d) % 4) for i in range(4)]) for d in (1, 2, 3)]
    mine, theirs = output(where, ctx, ow)
    return tuple(finish(mine, swap(theirs, "c"), residual, norm_gain.reshape(1, -1)))


def solution(mesh):
    fine = Mesh(mesh.devices.reshape(4, 4, 2, 2, 2, 2), (Z, X, "yh", "yl", "zl", "c"))
    seq = (X, "yh", "yl", "zl", "c")
    in_specs = (
        P(None, seq, Z),
        P(seq, Z),
        P(),
        P(seq, Z),
        P(Z, None),
        P(seq + (Z,), None),
        P(),
    )
    out_specs = (P(seq + (Z,), None), P(seq + (Z,), None))
    return jax.shard_map(shards, mesh=fine, in_specs=in_specs, out_specs=out_specs, check_vma=False)
```

time: 271 us -> 272 us (level)
  Pallas kernels: 35.7 us -> 47.4 us
  waiting for transfers between devices: 143 us -> 134 us
    pallas_call x4 -> x5, Pallas kernels: 21.4 us -> 33.1 us  [the longest x2 18.9 us: attend(): pl.pallas_call(functools.partial(attend_kernel, chunk, last), out_shape=o...]
    all_to_all x2, waiting for transfers between devices: 8.11 us -> 0.01 us  [shards(): lax.all_to_all(both.reshape(16, step, 512), (X, 'yh', 'c'), 0, 0, tiled=T...]
    ppermute x2, waiting for transfers between devices: 10.4 us -> 15.1 us  [shards(): opp_a = lax.ppermute(prev[:half], Z, FWD)]
    ppermute x14 -> x9, starting transfers between devices: 17.4 us -> 12.8 us  [swap(): return lax.ppermute(a, axis, [(0, 1), (1, 0)])]
    all_gather x1, waiting for transfers between devices: 40.8 us -> 36.7 us  [shards(): w_mine = lax.all_gather(rows, XY, axis=0, tiled=True)]
    ppermute x2, waiting for transfers between devices: 32.4 us -> 29.1 us  [shards(): opp_b = lax.ppermute(nxt[half:], Z, BWD)]
    ppermute x1, waiting for transfers between devices: 0.01 us -> 2.91 us  [shards(): w_zc = lax.ppermute(theirs, ('zl', 'c'), [(i, 3 - i) for i in range(4)])]
    ppermute x3, waiting for transfers between devices: 7.68 us -> 10.5 us  [shards(): lax.ppermute(ow, Z, [(i, (i + 4 - d) % 4) for i in range(4)])]
  transfers between devices with their start and end apart: 34 -> 29, of which waited for: 18 -> 16; matrix products, arithmetic and copies ran while one was open for 4% -> 3% of each run, Pallas kernels for 10% -> 13%
where the time goes in v1:
time: 272 us; the launch traced here: 271 us
  waiting for transfers between devices  134 us (49%)
  starting transfers between devices  61.5 us (23%)
  Pallas kernels  47.4 us (17%)
  between operations  14.3 us (5%)
  local copies, waits for them, and re-layouts  7.5 us (3%)
  other arithmetic  5.75 us (2%)
    all_gather x1, waiting for transfers between devices, shards(): w_mine = lax.all_gather(rows, XY, axis=0, tiled=True)  36.7 us
    ppermute x2, waiting for transfers between devices, shards(): opp_b = lax.ppermute(nxt[half:], Z, BWD)  29.1 us
    ppermute x2, waiting for transfers between devices, shards(): prev = lax.ppermute(own, Z, FWD)  19.5 us
    pallas_call x2, Pallas kernels, attend(): pl.pallas_call(functools.partial(attend_kernel, chunk, last), out_shape=o...  18.9 us
    ppermute x2, waiting for transfers between devices, shards(): opp_a = lax.ppermute(prev[:half], Z, FWD)  15.1 us
    pallas_call x2, Pallas kernels, project(): pl.pallas_call(project_kernel, out_shape=jax.ShapeDtypeStruct((8, 2, rows...  14.2 us
    all_to_all x2, starting transfers between devices, shards(): lax.all_to_all(both.reshape(16, step, 512), (X, 'yh', 'c'), 0, 0, tiled=T...  13.6 us
    ppermute x9, starting transfers between devices, swap(): return lax.ppermute(a, axis, [(0, 1), (1, 0)])  12.8 us
  transfers between devices with their start and end apart: 29, of which 16 were waited for; matrix products, arithmetic and copies ran while one was open for 3% of the time, Pallas kernels for 13%

profile of v1, /device:TPU:1, one launch (start us, length us, event | category | flops | bytes accessed | tf_op | source)
XLA Modules:
  0.0 270.9 jit_solution(6990091379392949209)
XLA Ops:
  7.2 1.0 broadcast_select_fusion.3
  8.2 3.3 %collective-permute-start.7 = (bf16[64,512]{1,0:T(8,128)(2,1)S(1)}, bf16[64,512]{1,0:T(8,128)(2,1)S(1)}, u32[]{:S(2)}, u32[]{:S(2)}) collective-permute-start(bf16[64,512]{1,0:T(8,128)(2,1)S(1)} %get-tuple-element.35), channel_id=1, source_target_pairs={{0,1},{1,0},{2,3},{3,2},{4,5},{5,4},{6,7},{7,6},{8,9},{9,8},{10,11... | collective-permute-start | bytes 196616 | tf_op jit(solution)/shard_map/ppermute | solution.py:25
  11.5 1.4 collective-permute-start.8
  13.0 2.9 %collective-permute-done.9 = bf16[64,512]{1,0:T(8,128)(2,1)S(1)} collective-permute-done((bf16[64,512]{1,0:T(8,128)(2,1)S(1)}, bf16[64,512]{1,0:T(8,128)(2,1)S(1)}, u32[]{:S(2)}, u32[]{:S(2)}) %collective-permute-start.9) | collective-permute-done | bytes 65568 | tf_op jit(solution)/shard_map/ppermute | solution.py:240
  17.3 0.9 dynamic_slice.8
  18.2 1.2 collective-permute-start.12
  19.4 5.3 %collective-permute-start.11 = (bf16[256,256]{1,0:T(8,128)(2,1)S(1)}, bf16[256,256]{1,0:T(8,128)(2,1)S(1)}, u32[]{:S(2)}, u32[]{:S(2)}) collective-permute-start(bf16[256,256]{1,0:T(8,128)(2,1)S(1)} %dynamic_slice.8), channel_id=1, source_target_pairs={{0,128},{64,192},{128,0},{192,64},{1,129},{65,193},{129,1},{193,65... | collective-permute-start | bytes 393224 | tf_op jit(solution)/shard_map/ppermute | solution.py:256
  24.7 2.4 collective-permute-start.10
  27.1 5.4 %collective-permute-done.11 = bf16[256,256]{1,0:T(8,128)(2,1)S(1)} collective-permute-done((bf16[256,256]{1,0:T(8,128)(2,1)S(1)}, bf16[256,256]{1,0:T(8,128)(2,1)S(1)}, u32[]{:S(2)}, u32[]{:S(2)}) %collective-permute-start.11) | collective-permute-done | bytes 131104 | tf_op jit(solution)/shard_map/ppermute | solution.py:256
  32.4 5.2 %collective-permute-done.10 = bf16[256,256]{1,0:T(8,128)(2,1)S(1)} collective-permute-done((bf16[256,256]{1,0:T(8,128)(2,1)S(1)}, bf16[256,256]{1,0:T(8,128)(2,1)S(1)}, u32[]{:S(2)}, u32[]{:S(2)}) %collective-permute-start.10) | collective-permute-done | bytes 131104 | tf_op jit(solution)/shard_map/ppermute | solution.py:256
  37.6 0.9 pad_maximum_fusion
  38.5 36.7 %all-gather.3.cloned.1.call-done.w_mine = bf16[4096,512]{1,0:T(8,128)(2,1)} async-done(((bf16[256,512]{1,0:T(8,128)(2,1)}), bf16[4096,512]{1,0:T(8,128)(2,1)}) %all-gather.3.cloned.1.call-update) | async-done | bytes 4194320 | tf_op jit(solution)/shard_map/all_gather | solution.py:242
  75.2 0.9 collective-permute-start.13
  76.3 2.3 collective-permute-start.15
  78.6 1.7 collective-permute-start.14
  80.3 19.5 %collective-permute-done.15.prev = bf16[256,1024]{1,0:T(8,128)(2,1)S(1)} collective-permute-done((bf16[256,1024]{1,0:T(8,128)(2,1)S(1)}, bf16[256,1024]{1,0:T(8,128)(2,1)S(1)}, u32[]{:S(2)}, u32[]{:S(2)}) %collective-permute-start.15) | collective-permute-done | bytes 524320 | tf_op jit(solution)/shard_map/ppermute | solution.py:249
  99.8 4.8 %collective-permute-start.16 = (bf16[128,1024]{1,0:T(8,128)(2,1)S(1)}, bf16[128,1024]{1,0:T(8,128)(2,1)}, u32[]{:S(2)}, u32[]{:S(2)}) collective-permute-start(bf16[128,1024]{1,0:T(8,128)(2,1)S(1)} %slice.46), channel_id=1, source_target_pairs={{0,64},{64,128},{128,192},{192,0},{1,65},{65,129},{129,193},{193,1... | collective-permute-start | bytes 786440 | tf_op jit(solution)/shard_map/ppermute | solution.py:251
  104.6 1.3 collective-permute-start
  105.9 4.4 %collective-permute-start.4 = (bf16[256,1024]{1,0:T(8,128)(2,1)S(1)}, bf16[256,1024]{1,0:T(8,128)(2,1)S(1)}, u32[]{:S(2)}, u32[]{:S(2)}) collective-permute-start(bf16[256,1024]{1,0:T(8,128)(2,1)S(1)} %bitcast.19), channel_id=1, source_target_pairs={{0,64},{64,128},{128,192},{192,0},{1,65},{65,129},{129,193},{193,1... | collective-permute-start | bytes 1572872 | tf_op jit(solution)/shard_map/ppermute | solution.py:249
  111.2 4.4 %collective-permute-done.16.opp_a = bf16[128,1024]{1,0:T(8,128)(2,1)} collective-permute-done((bf16[128,1024]{1,0:T(8,128)(2,1)S(1)}, bf16[128,1024]{1,0:T(8,128)(2,1)}, u32[]{:S(2)}, u32[]{:S(2)}) %collective-permute-start.16) | collective-permute-done | bytes 262176 | tf_op jit(solution)/shard_map/ppermute | solution.py:251
  115.6 1.7 collective-permute-start.1
  117.9 26.6 %collective-permute-done.17.opp_b = bf16[128,1024]{1,0:T(8,128)(2,1)} collective-permute-done((bf16[128,1024]{1,0:T(8,128)(2,1)}, bf16[128,1024]{1,0:T(8,128)(2,1)}, u32[]{:S(2)}, u32[]{:S(2)}) %collective-permute-start.17) | collective-permute-done | bytes 262176 | tf_op jit(solution)/shard_map/ppermute | solution.py:252
  144.5 7.1 %project.3 = bf16[8,2,32,512]{3,2,1,0:T(8,128)(2,1)} custom-call(s32[4]{0:T(128)} %pad_add_fusion.where_ref, bf16[256,1024]{1,0:T(8,128)(2,1)} %bitcast.24, bf16[256,1024]{1,0:T(8,128)(2,1)} %copy-done.7, bf16[128,1024]{1,0:T(8,128)(2,1)} %collective-permute-done.16.opp_a, bf16[128,1024]{1,0:T(8,128)(2,1)} %collective-permute-done.17.opp_b, ...), custom_call_target="tpu_custom_call" | custom-call | tf_op jit(solution)/shard_map/project/pallas_call | solution.py:61
  151.6 5.6 %all-to-all-start.1 = ((bf16[16,32,512]{2,1,0:T(8,128)(2,1)}), bf16[16,32,512]{2,1,0:T(8,128)(2,1)S(1)}, u32[]{:S(2)}, u32[]{:S(2)}) async-start(bf16[16,32,512]{2,1,0:T(8,128)(2,1)} %bitcast.17), calls=%async_computation.1 | async-start | bytes 1048576 | tf_op jit(solution)/shard_map/all_to_all | solution.py:275
  157.2 1.2 maximum_select_fusion.1
  158.8 4.5 %collective-permute-start.5 = (bf16[128,1024]{1,0:T(8,128)(2,1)S(1)}, bf16[128,1024]{1,0:T(8,128)(2,1)S(1)}, u32[]{:S(2)}, u32[]{:S(2)}) collective-permute-start(bf16[128,1024]{1,0:T(8,128)(2,1)S(1)} %slice.44), channel_id=1, source_target_pairs={{0,64},{64,128},{128,192},{192,0},{1,65},{65,129},{129,193},{193,1... | collective-permute-start | bytes 786440 | tf_op jit(solution)/shard_map/ppermute | solution.py:251
  163.4 10.7 %collective-permute-done.5.opp_a = bf16[128,1024]{1,0:T(8,128)(2,1)S(1)} collective-permute-done((bf16[128,1024]{1,0:T(8,128)(2,1)S(1)}, bf16[128,1024]{1,0:T(8,128)(2,1)S(1)}, u32[]{:S(2)}, u32[]{:S(2)}) %collective-permute-start.5) | collective-permute-done | bytes 262176 | tf_op jit(solution)/shard_map/ppermute | solution.py:251
  174.1 2.5 collective-permute-done.6.opp_b
  177.3 7.1 %project.2 = bf16[8,2,32,512]{3,2,1,0:T(8,128)(2,1)} custom-call(s32[4]{0:T(128)} %pad_add_fusion.where_ref, bf16[256,1024]{1,0:T(8,128)(2,1)} %bitcast.20, bf16[256,1024]{1,0:T(8,128)(2,1)} %copy-done.4, bf16[128,1024]{1,0:T(8,128)(2,1)} %copy-done.13, bf16[128,1024]{1,0:T(8,128)(2,1)} %copy-done.14, bf16[256,1024]{1,0:T(8,128)(2,1)} %copy-done.5, ...), custom_call_target="tpu_custom_call" | custom-call | tf_op jit(solution)/shard_map/project/pallas_call | solution.py:61
  184.4 7.9 %all-to-all-start = ((bf16[16,32,512]{2,1,0:T(8,128)(2,1)}), bf16[16,32,512]{2,1,0:T(8,128)(2,1)S(1)}, u32[]{:S(2)}, u32[]{:S(2)}) async-start(bf16[16,32,512]{2,1,0:T(8,128)(2,1)} %bitcast.16), calls=%async_computation | async-start | bytes 1048576 | tf_op jit(solution)/shard_map/all_to_all | solution.py:275
  192.9 1.2 stack.44.where_ref
  194.2 1.2 maximum_select_fusion.q_ref
  195.4 9.1 %attend.2 = (f32[8,256,256]{2,1,0:T(8,128)}, f32[8,8,256]{2,1,0:T(8,128)}) custom-call(s32[6]{0:T(128)} %stack.44.where_ref, bf16[2048,256]{1,0:T(8,128)(2,1)} %maximum_select_fusion.q_ref, bf16[512,512]{1,0:T(8,128)(2,1)} %bitcast.21), custom_call_target="tpu_custom_call" | custom-call | tf_op jit(solution)/shard_map/attend/pallas_call | solution.py:139
  204.5 0.8 copy-done.3
  205.3 9.8 %attend.3 = (bf16[2,272,256]{2,1,0:T(8,128)(2,1)}, bf16[2,272,256]{2,1,0:T(8,128)(2,1)}, bf16[2,272,256]{2,1,0:T(8,128)(2,1)}, bf16[2,272,256]{2,1,0:T(8,128)(2,1)}) custom-call(s32[6]{0:T(128)} %stack.44.where_ref, bf16[2048,256]{1,0:T(8,128)(2,1)} %maximum_select_fusion.q_ref, bf16[512,512]{1,0:T(8,128)(2,1)} %bitcast.25, ...), custom_call_target="tpu_custom_call" | custom-call | tf_op jit(solution)/shard_map/attend/pallas_call | solution.py:139
  215.3 2.5 collective-permute-start.20
  217.8 5.5 %collective-permute-done.18.b_ref = bf16[2,272,256]{2,1,0:T(8,128)(2,1)S(1)} collective-permute-done((bf16[2,272,256]{2,1,0:T(8,128)(2,1)}, bf16[2,272,256]{2,1,0:T(8,128)(2,1)S(1)}, u32[]{:S(2)}, u32[]{:S(2)}) %collective-permute-start.18) | collective-permute-done | bytes 278560 | tf_op jit(solution)/shard_map/ppermute | solution.py:25
  223.7 5.3 %collective-permute-done.20.d_ref = bf16[2,272,256]{2,1,0:T(8,128)(2,1)S(1)} collective-permute-done((bf16[2,272,256]{2,1,0:T(8,128)(2,1)}, bf16[2,272,256]{2,1,0:T(8,128)(2,1)S(1)}, u32[]{:S(2)}, u32[]{:S(2)}) %collective-permute-start.20) | collective-permute-done | bytes 278560 | tf_op jit(solution)/shard_map/ppermute | solution.py:283
  229.8 2.3 merge.1
  232.1 2.4 collective-permute-start.21
  234.5 3.6 %collective-permute-start.22 = (bf16[128,256]{1,0:T(8,128)(2,1)}, bf16[128,256]{1,0:T(8,128)(2,1)S(1)}, u32[]{:S(2)}, u32[]{:S(2)}) collective-permute-start(bf16[128,256]{1,0:T(8,128)(2,1)} %get-tuple-element.25), channel_id=1, source_target_pairs={{0,128},{64,192},{128,0},{192,64},{1,129},{65,193},{129,1},{193,65... | collective-permute-start | bytes 196616 | tf_op jit(solution)/shard_map/ppermute | solution.py:286
  238.1 4.4 %collective-permute-done.22.refs_2_ = bf16[128,256]{1,0:T(8,128)(2,1)S(1)} collective-permute-done((bf16[128,256]{1,0:T(8,128)(2,1)}, bf16[128,256]{1,0:T(8,128)(2,1)S(1)}, u32[]{:S(2)}, u32[]{:S(2)}) %collective-permute-start.22) | collective-permute-done | bytes 65568 | tf_op jit(solution)/shard_map/ppermute | solution.py:286
  242.5 1.8 collective-permute-done.23.refs_3_
  244.9 8.1 %output.1 = (f32[64,4096]{1,0:T(8,128)}, f32[64,4096]{1,0:T(8,128)}) custom-call(s32[4]{0:T(128)} %pad_add_fusion.where_ref, bf16[128,256]{1,0:T(8,128)(2,1)} %get-tuple-element.23.refs_0_, bf16[128,256]{1,0:T(8,128)(2,1)} %copy-done.16, bf16[128,256]{1,0:T(8,128)(2,1)} %copy-done.17, bf16[128,256]{1,0:T(8,128)(2,1)} %copy-done.18, ...), custom_call_target="tpu_custom_call" | custom-call | tf_op jit(solution)/shard_map/output/pallas_call | solution.py:202
  253.0 3.7 %collective-permute-start.24 = (f32[64,4096]{1,0:T(8,128)}, f32[64,4096]{1,0:T(8,128)S(1)}, u32[]{:S(2)}, u32[]{:S(2)}) collective-permute-start(f32[64,4096]{1,0:T(8,128)} %get-tuple-element.29), channel_id=1, source_target_pairs={{0,1},{1,0},{2,3},{3,2},{4,5},{5,4},{6,7},{7,6},{8,9},{9,8},{10,11... | collective-permute-start | bytes 3145736 | tf_op jit(solution)/shard_map/ppermute | solution.py:25
  256.7 2.5 collective-permute-done.24.other
  259.2 1.0 copy-done.9
  260.2 3.8 %finish.1 = (bf16[64,4096]{1,0:T(8,128)(2,1)}, bf16[64,4096]{1,0:T(8,128)(2,1)}) custom-call(f32[64,4096]{1,0:T(8,128)} %get-tuple-element.28.mine, f32[64,4096]{1,0:T(8,128)} %copy-done.9, bf16[64,4096]{1,0:T(8,128)(2,1)} %residual.1, f32[1,4096]{1,0:T(1,128)} %bitcast.26), custom_call_target="tpu_custom_call" | custom-call | tf_op jit(solution)/shard_map/finish/pallas_call | solution.py:221
  (77 shorter events, 6.6 us)
Async XLA Ops:
  7.2 69.0 %copy-start.8 = (bf16[8,64,1024]{2,1,0:T(8,128)(2,1)S(1)}, bf16[8,64,1024]{2,1,0:T(8,128)(2,1)}, u32[]{:S(2)}) copy-start(bf16[8,64,1024]{2,1,0:T(8,128)(2,1)} %param.7) | copy-start | bytes 3145732
  7.2 68.0 %all-gather.3.cloned.1.call-start = ((), (), s32[]{:S(2)}) async-start(), calls=%async_computation.2 | async-start | bytes 4456448 | tf_op jit(solution)/shard_map/all_gather | solution.py:242
  8.2 4.7 %collective-permute-start.7 = (bf16[64,512]{1,0:T(8,128)(2,1)S(1)}, bf16[64,512]{1,0:T(8,128)(2,1)S(1)}, u32[]{:S(2)}, u32[]{:S(2)}) collective-permute-start(bf16[64,512]{1,0:T(8,128)(2,1)S(1)} %get-tuple-element.35), channel_id=1, source_target_pairs={{0,1},{1,0},{2,3},{3,2},{4,5},{5,4},{6,7},{7,6},{8,9},{9,8},{10,11... | collective-permute-start | bytes 196616 | tf_op jit(solution)/shard_map/ppermute | solution.py:25
  11.5 4.4 %collective-permute-start.9 = (bf16[64,512]{1,0:T(8,128)(2,1)S(1)}, bf16[64,512]{1,0:T(8,128)(2,1)S(1)}, u32[]{:S(2)}, u32[]{:S(2)}) collective-permute-start(bf16[64,512]{1,0:T(8,128)(2,1)S(1)} %get-tuple-element.35), channel_id=1, source_target_pairs={{0,3},{1,2},{2,1},{3,0},{4,7},{5,6},{6,5},{7,4},{8,11},{9,10},{10,... | collective-permute-start | bytes 196616 | tf_op jit(solution)/shard_map/ppermute | solution.py:240
  11.5 4.9 %collective-permute-start.8 = (bf16[64,512]{1,0:T(8,128)(2,1)S(1)}, bf16[64,512]{1,0:T(8,128)(2,1)S(1)}, u32[]{:S(2)}, u32[]{:S(2)}) collective-permute-start(bf16[64,512]{1,0:T(8,128)(2,1)S(1)} %get-tuple-element.34), channel_id=1, source_target_pairs={{0,2},{2,0},{1,3},{3,1},{4,6},{6,4},{5,7},{7,5},{8,10},{10,8},{9,1... | collective-permute-start | bytes 196616 | tf_op jit(solution)/shard_map/ppermute | solution.py:25
  17.2 227.1 %all-gather.5.cloned.1.call-start = ((), (), s32[]{:S(2)}) async-start(), calls=%async_computation.3 | async-start | bytes 8912896 | tf_op jit(solution)/shard_map/all_gather | solution.py:260
  18.2 86.4 %copy-start.15 = (bf16[256,512]{1,0:T(8,128)(2,1)S(1)}, bf16[256,512]{1,0:T(8,128)(2,1)}, u32[]{:S(2)}) copy-start(bf16[256,512]{1,0:T(8,128)(2,1)} %param.10) | copy-start | bytes 786436
  18.2 8.9 %collective-permute-start.12 = (bf16[256,256]{1,0:T(8,128)(2,1)S(1)}, bf16[256,256]{1,0:T(8,128)(2,1)S(1)}, u32[]{:S(2)}, u32[]{:S(2)}) collective-permute-start(bf16[256,256]{1,0:T(8,128)(2,1)S(1)} %dynamic_slice.8), channel_id=1, source_target_pairs={{0,64},{64,128},{128,192},{192,0},{1,65},{65,129},{129,193},{193,1... | collective-permute-start | bytes 393224 | tf_op jit(solution)/shard_map/ppermute | solution.py:256
  19.4 13.0 %collective-permute-start.11 = (bf16[256,256]{1,0:T(8,128)(2,1)S(1)}, bf16[256,256]{1,0:T(8,128)(2,1)S(1)}, u32[]{:S(2)}, u32[]{:S(2)}) collective-permute-start(bf16[256,256]{1,0:T(8,128)(2,1)S(1)} %dynamic_slice.8), channel_id=1, source_target_pairs={{0,128},{64,192},{128,0},{192,64},{1,129},{65,193},{129,1},{193,65... | collective-permute-start | bytes 393224 | tf_op jit(solution)/shard_map/ppermute | solution.py:256
  24.7 12.9 %collective-permute-start.10 = (bf16[256,256]{1,0:T(8,128)(2,1)S(1)}, bf16[256,256]{1,0:T(8,128)(2,1)S(1)}, u32[]{:S(2)}, u32[]{:S(2)}) collective-permute-start(bf16[256,256]{1,0:T(8,128)(2,1)S(1)} %dynamic_slice.8), channel_id=1, source_target_pairs={{0,192},{64,0},{128,64},{192,128},{1,193},{65,1},{129,65},{193,129... | collective-permute-start | bytes 393224 | tf_op jit(solution)/shard_map/ppermute | solution.py:256
  75.2 69.2 %collective-permute-start.13 = (bf16[4096,512]{1,0:T(8,128)(2,1)}, bf16[4096,512]{1,0:T(8,128)(2,1)}, u32[]{:S(2)}, u32[]{:S(2)}) collective-permute-start(bf16[4096,512]{1,0:T(8,128)(2,1)} %all-gather.3.cloned.1.call-done.w_mine), channel_id=1, source_target_pairs={{0,1},{1,0},{2,3},{3,2},{4,5},{5,4},{6,7},{7,6},{8,9},{9,8},{10,11... | collective-permute-start | bytes 12582920 | tf_op jit(solution)/shard_map/ppermute | solution.py:25
  76.2 68.2 %copy-start.2 = (bf16[8,32,1024]{2,1,0:T(8,128)(2,1)}, bf16[8,32,1024]{2,1,0:T(8,128)(2,1)S(1)}, u32[]{:S(2)}) copy-start(bf16[8,32,1024]{2,1,0:T(8,128)(2,1)S(1)} %get-tuple-element.30) | copy-start | bytes 1572868
  76.3 75.4 %copy-start = (bf16[8,32,1024]{2,1,0:T(8,128)(2,1)}, bf16[8,32,1024]{2,1,0:T(8,128)(2,1)S(1)}, u32[]{:S(2)}) copy-start(bf16[8,32,1024]{2,1,0:T(8,128)(2,1)S(1)} %get-tuple-element.31) | copy-start | bytes 1572868
  76.3 23.5 %collective-permute-start.15 = (bf16[256,1024]{1,0:T(8,128)(2,1)S(1)}, bf16[256,1024]{1,0:T(8,128)(2,1)S(1)}, u32[]{:S(2)}, u32[]{:S(2)}) collective-permute-start(bf16[256,1024]{1,0:T(8,128)(2,1)S(1)} %bitcast.22), channel_id=1, source_target_pairs={{0,64},{64,128},{128,192},{192,0},{1,65},{65,129},{129,193},{193,1... | collective-permute-start | bytes 1572872 | tf_op jit(solution)/shard_map/ppermute | solution.py:249
  78.6 27.3 %collective-permute-start.14 = (bf16[256,1024]{1,0:T(8,128)(2,1)S(1)}, bf16[256,1024]{1,0:T(8,128)(2,1)S(1)}, u32[]{:S(2)}, u32[]{:S(2)}) collective-permute-start(bf16[256,1024]{1,0:T(8,128)(2,1)S(1)} %bitcast.23), channel_id=1, source_target_pairs={{0,192},{64,0},{128,64},{192,128},{1,193},{65,1},{129,65},{193,129... | collective-permute-start | bytes 1572872 | tf_op jit(solution)/shard_map/ppermute | solution.py:250
  99.8 44.7 %copy-start.6 = (bf16[256,1024]{1,0:T(8,128)(2,1)}, bf16[256,1024]{1,0:T(8,128)(2,1)S(1)}, u32[]{:S(2)}) copy-start(bf16[256,1024]{1,0:T(8,128)(2,1)S(1)} %collective-permute-done.15.prev) | copy-start | bytes 1572868
  99.8 15.8 %collective-permute-start.16 = (bf16[128,1024]{1,0:T(8,128)(2,1)S(1)}, bf16[128,1024]{1,0:T(8,128)(2,1)}, u32[]{:S(2)}, u32[]{:S(2)}) collective-permute-start(bf16[128,1024]{1,0:T(8,128)(2,1)S(1)} %slice.46), channel_id=1, source_target_pairs={{0,64},{64,128},{128,192},{192,0},{1,65},{65,129},{129,193},{193,1... | collective-permute-start | bytes 786440 | tf_op jit(solution)/shard_map/ppermute | solution.py:251
  104.6 6.4 %collective-permute-start = (bf16[256,256]{1,0:T(8,128)(2,1)S(1)}, bf16[256,256]{1,0:T(8,128)(2,1)S(1)}, u32[]{:S(2)}, u32[]{:S(2)}) collective-permute-start(bf16[256,256]{1,0:T(8,128)(2,1)S(1)} %get-tuple-element.33), channel_id=1, source_target_pairs={{0,1},{1,0},{2,3},{3,2},{4,5},{5,4},{6,7},{7,6},{8,9},{9,8},{10,11... | collective-permute-start | bytes 393224 | tf_op jit(solution)/shard_map/ppermute | solution.py:25
  105.9 57.4 %collective-permute-start.3 = (bf16[256,1024]{1,0:T(8,128)(2,1)S(1)}, bf16[256,1024]{1,0:T(8,128)(2,1)S(1)}, u32[]{:S(2)}, u32[]{:S(2)}) collective-permute-start(bf16[256,1024]{1,0:T(8,128)(2,1)S(1)} %bitcast.18), channel_id=1, source_target_pairs={{0,192},{64,0},{128,64},{192,128},{1,193},{65,1},{129,65},{193,129... | collective-permute-start | bytes 1572872 | tf_op jit(solution)/shard_map/ppermute | solution.py:250
  105.9 38.5 %copy-start.7 = (bf16[256,1024]{1,0:T(8,128)(2,1)}, bf16[256,1024]{1,0:T(8,128)(2,1)S(1)}, u32[]{:S(2)}) copy-start(bf16[256,1024]{1,0:T(8,128)(2,1)S(1)} %collective-permute-done.14.nxt) | copy-start | bytes 1572868
  105.9 52.8 %collective-permute-start.4 = (bf16[256,1024]{1,0:T(8,128)(2,1)S(1)}, bf16[256,1024]{1,0:T(8,128)(2,1)S(1)}, u32[]{:S(2)}, u32[]{:S(2)}) collective-permute-start(bf16[256,1024]{1,0:T(8,128)(2,1)S(1)} %bitcast.19), channel_id=1, source_target_pairs={{0,64},{64,128},{128,192},{192,0},{1,65},{65,129},{129,193},{193,1... | collective-permute-start | bytes 1572872 | tf_op jit(solution)/shard_map/ppermute | solution.py:249
  111.0 33.4 %collective-permute-start.17 = (bf16[128,1024]{1,0:T(8,128)(2,1)}, bf16[128,1024]{1,0:T(8,128)(2,1)}, u32[]{:S(2)}, u32[]{:S(2)}) collective-permute-start(bf16[128,1024]{1,0:T(8,128)(2,1)} %slice.47), channel_id=1, source_target_pairs={{0,192},{64,0},{128,64},{192,128},{1,193},{65,1},{129,65},{193,129... | collective-permute-start | bytes 786440 | tf_op jit(solution)/shard_map/ppermute | solution.py:252
  115.6 41.7 %collective-permute-start.1 = (bf16[512,256]{1,0:T(8,128)(2,1)S(1)}, bf16[512,256]{1,0:T(8,128)(2,1)}, u32[]{:S(2)}, u32[]{:S(2)}) collective-permute-start(bf16[512,256]{1,0:T(8,128)(2,1)S(1)} %maximum_select_fusion.2), channel_id=1, source_target_pairs={{0,2},{2,0},{1,3},{3,1},{4,6},{6,4},{5,7},{7,5},{8,10},{10,8},{9,1... | collective-permute-start | bytes 786440 | tf_op jit(solution)/shard_map/ppermute | solution.py:25
  151.6 32.8 %all-to-all-start.1 = ((bf16[16,32,512]{2,1,0:T(8,128)(2,1)}), bf16[16,32,512]{2,1,0:T(8,128)(2,1)S(1)}, u32[]{:S(2)}, u32[]{:S(2)}) async-start(bf16[16,32,512]{2,1,0:T(8,128)(2,1)} %bitcast.17), calls=%async_computation.1 | async-start | bytes 1048576 | tf_op jit(solution)/shard_map/all_to_all | solution.py:275
  158.5 35.7 %collective-permute-start.2 = (bf16[1024,256]{1,0:T(8,128)(2,1)S(1)}, bf16[1024,256]{1,0:T(8,128)(2,1)S(1)}, u32[]{:S(2)}, u32[]{:S(2)}) collective-permute-start(bf16[1024,256]{1,0:T(8,128)(2,1)S(1)} %maximum_select_fusion.1), channel_id=1, source_target_pairs={{0,4},{4,0},{1,5},{5,1},{2,6},{6,2},{3,7},{7,3},{8,12},{12,8},{9,1... | collective-permute-start | bytes 1572872 | tf_op jit(solution)/shard_map/ppermute | solution.py:25
  158.7 17.9 %copy-start.5 = (bf16[256,1024]{1,0:T(8,128)(2,1)}, bf16[256,1024]{1,0:T(8,128)(2,1)S(1)}, u32[]{:S(2)}) copy-start(bf16[256,1024]{1,0:T(8,128)(2,1)S(1)} %collective-permute-done.4.prev) | copy-start | bytes 1572868
  158.8 15.3 %collective-permute-start.5 = (bf16[128,1024]{1,0:T(8,128)(2,1)S(1)}, bf16[128,1024]{1,0:T(8,128)(2,1)S(1)}, u32[]{:S(2)}, u32[]{:S(2)}) collective-permute-start(bf16[128,1024]{1,0:T(8,128)(2,1)S(1)} %slice.44), channel_id=1, source_target_pairs={{0,64},{64,128},{128,192},{192,0},{1,65},{65,129},{129,193},{193,1... | collective-permute-start | bytes 786440 | tf_op jit(solution)/shard_map/ppermute | solution.py:251
  163.3 13.3 %copy-start.4 = (bf16[256,1024]{1,0:T(8,128)(2,1)}, bf16[256,1024]{1,0:T(8,128)(2,1)S(1)}, u32[]{:S(2)}) copy-start(bf16[256,1024]{1,0:T(8,128)(2,1)S(1)} %collective-permute-done.3.nxt) | copy-start | bytes 1572868
  163.3 29.0 %copy-start.19 = (s32[8]{0:T(128)S(1)}, s32[8]{0:T(128)}, u32[]{:S(2)}) copy-start(s32[8]{0:T(128)} %param.9) | copy-start | bytes 100
  163.3 13.3 %collective-permute-start.6 = (bf16[128,1024]{1,0:T(8,128)(2,1)S(1)}, bf16[128,1024]{1,0:T(8,128)(2,1)S(1)}, u32[]{:S(2)}, u32[]{:S(2)}) collective-permute-start(bf16[128,1024]{1,0:T(8,128)(2,1)S(1)} %slice.45), channel_id=1, source_target_pairs={{0,192},{64,0},{128,64},{192,128},{1,193},{65,1},{129,65},{193,129... | collective-permute-start | bytes 786440 | tf_op jit(solution)/shard_map/ppermute | solution.py:252
  174.1 2.5 copy-start.13
  176.6 0.7 copy-start.14
  184.4 11.0 %copy-start.1 = (bf16[16,32,512]{2,1,0:T(8,128)(2,1)}, bf16[16,32,512]{2,1,0:T(8,128)(2,1)S(1)}, u32[]{:S(2)}) copy-start(bf16[16,32,512]{2,1,0:T(8,128)(2,1)S(1)} %all-to-all-done.1) | copy-start | bytes 1572868
  184.4 20.1 %all-to-all-start = ((bf16[16,32,512]{2,1,0:T(8,128)(2,1)}), bf16[16,32,512]{2,1,0:T(8,128)(2,1)S(1)}, u32[]{:S(2)}, u32[]{:S(2)}) async-start(bf16[16,32,512]{2,1,0:T(8,128)(2,1)} %bitcast.16), calls=%async_computation | async-start | bytes 1048576 | tf_op jit(solution)/shard_map/all_to_all | solution.py:275
  204.5 0.8 copy-start.3
  215.1 8.2 %collective-permute-start.18 = (bf16[2,272,256]{2,1,0:T(8,128)(2,1)}, bf16[2,272,256]{2,1,0:T(8,128)(2,1)S(1)}, u32[]{:S(2)}, u32[]{:S(2)}) collective-permute-start(bf16[2,272,256]{2,1,0:T(8,128)(2,1)} %get-tuple-element.20), channel_id=1, source_target_pairs={{0,2},{2,0},{1,3},{3,1},{4,6},{6,4},{5,7},{7,5},{8,10},{10,8},{9,1... | collective-permute-start | bytes 835592 | tf_op jit(solution)/shard_map/ppermute | solution.py:25
  215.1 8.6 %collective-permute-start.19 = (bf16[2,272,256]{2,1,0:T(8,128)(2,1)}, bf16[2,272,256]{2,1,0:T(8,128)(2,1)S(1)}, u32[]{:S(2)}, u32[]{:S(2)}) collective-permute-start(bf16[2,272,256]{2,1,0:T(8,128)(2,1)} %get-tuple-element.21), channel_id=1, source_target_pairs={{0,4},{4,0},{1,5},{5,1},{2,6},{6,2},{3,7},{7,3},{8,12},{12,8},{9,1... | collective-permute-start | bytes 835592 | tf_op jit(solution)/shard_map/ppermute | solution.py:25
  215.3 13.8 %collective-permute-start.20 = (bf16[2,272,256]{2,1,0:T(8,128)(2,1)}, bf16[2,272,256]{2,1,0:T(8,128)(2,1)S(1)}, u32[]{:S(2)}, u32[]{:S(2)}) collective-permute-start(bf16[2,272,256]{2,1,0:T(8,128)(2,1)} %get-tuple-element.22), channel_id=1, source_target_pairs={{0,6},{2,4},{4,2},{6,0},{1,7},{3,5},{5,3},{7,1},{8,14},{10,12},{12... | collective-permute-start | bytes 835592 | tf_op jit(solution)/shard_map/ppermute | solution.py:283
  223.3 5.8 %copy-start.10 = (bf16[2,272,256]{2,1,0:T(8,128)(2,1)}, bf16[2,272,256]{2,1,0:T(8,128)(2,1)S(1)}, u32[]{:S(2)}) copy-start(bf16[2,272,256]{2,1,0:T(8,128)(2,1)S(1)} %collective-permute-done.18.b_ref) | copy-start | bytes 835588
  223.7 5.3 %copy-start.11 = (bf16[2,272,256]{2,1,0:T(8,128)(2,1)}, bf16[2,272,256]{2,1,0:T(8,128)(2,1)S(1)}, u32[]{:S(2)}) copy-start(bf16[2,272,256]{2,1,0:T(8,128)(2,1)S(1)} %collective-permute-done.19.c_ref) | copy-start | bytes 835588
  229.1 0.7 copy-start.12
  232.1 6.0 %collective-permute-start.21 = (bf16[128,256]{1,0:T(8,128)(2,1)}, bf16[128,256]{1,0:T(8,128)(2,1)S(1)}, u32[]{:S(2)}, u32[]{:S(2)}) collective-permute-start(bf16[128,256]{1,0:T(8,128)(2,1)} %get-tuple-element.24), channel_id=1, source_target_pairs={{0,192},{64,0},{128,64},{192,128},{1,193},{65,1},{129,65},{193,129... | collective-permute-start | bytes 196616 | tf_op jit(solution)/shard_map/ppermute | solution.py:286
  234.5 8.0 %collective-permute-start.22 = (bf16[128,256]{1,0:T(8,128)(2,1)}, bf16[128,256]{1,0:T(8,128)(2,1)S(1)}, u32[]{:S(2)}, u32[]{:S(2)}) collective-permute-start(bf16[128,256]{1,0:T(8,128)(2,1)} %get-tuple-element.25), channel_id=1, source_target_pairs={{0,128},{64,192},{128,0},{192,64},{1,129},{65,193},{129,1},{193,65... | collective-permute-start | bytes 196616 | tf_op jit(solution)/shard_map/ppermute | solution.py:286
  238.1 6.2 %collective-permute-start.23 = (bf16[128,256]{1,0:T(8,128)(2,1)}, bf16[128,256]{1,0:T(8,128)(2,1)S(1)}, u32[]{:S(2)}, u32[]{:S(2)}) collective-permute-start(bf16[128,256]{1,0:T(8,128)(2,1)} %get-tuple-element.26), channel_id=1, source_target_pairs={{0,64},{64,128},{128,192},{192,0},{1,65},{65,129},{129,193},{193,1... | collective-permute-start | bytes 196616 | tf_op jit(solution)/shard_map/ppermute | solution.py:286
  238.1 6.2 %copy-start.16 = (bf16[128,256]{1,0:T(8,128)(2,1)}, bf16[128,256]{1,0:T(8,128)(2,1)S(1)}, u32[]{:S(2)}) copy-start(bf16[128,256]{1,0:T(8,128)(2,1)S(1)} %collective-permute-done.21.refs_1_) | copy-start | bytes 196612
  242.5 1.8 copy-start.17
  253.0 6.2 %collective-permute-start.24 = (f32[64,4096]{1,0:T(8,128)}, f32[64,4096]{1,0:T(8,128)S(1)}, u32[]{:S(2)}, u32[]{:S(2)}) collective-permute-start(f32[64,4096]{1,0:T(8,128)} %get-tuple-element.29), channel_id=1, source_target_pairs={{0,1},{1,0},{2,3},{3,2},{4,5},{5,4},{6,7},{7,6},{8,9},{9,8},{10,11... | collective-permute-start | bytes 3145736 | tf_op jit(solution)/shard_map/ppermute | solution.py:25
  259.2 1.0 copy-start.9
  (1 other events, 0.6 us)
Sparse Core Ops, SparseCore 0:
  17.3 57.8 all-gather.2
  77.6 80.7 all-gather.4

commit v2 on v1

v2 whole, which is shorter than its diff:
```python
import functools
import math

import jax
import jax.numpy as jnp
from jax import lax
from jax.experimental import pallas as pl
from jax.experimental.pallas import tpu as pltpu
from jax.sharding import Mesh, PartitionSpec as P


DH = 256
CHUNKS = 2
VMEM_LIMIT = 16 << 20
BF = jnp.bfloat16
F32 = jnp.float32
X = "x"
XY = ("x", "yh", "yl")
Z = "zh"
EXP_SCALE = math.log2(math.e) / math.sqrt(DH)
FWD = [(i, (i + 1) % 4) for i in range(4)]
BWD = [(i, (i + 3) % 4) for i in range(4)]


def swap(a, axis):
    return lax.ppermute(a, axis, [(0, 1), (1, 0)])


def pair(a, b, index, axis=0):
    return jnp.where(index == 0, jnp.concatenate([a, b], axis), jnp.concatenate([b, a], axis))


def pick(a, b, index):
    return jnp.where(index == 0, a, b)


def kernel_call(kernel, outs, where, *args):
    spec = pl.BlockSpec(memory_space=pltpu.VMEM)
    args = [pltpu.with_memory_space_constraint(a, pltpu.VMEM) for a in args]
    return pl.pallas_call(
        kernel,
        out_shape=outs,
        in_specs=[pl.BlockSpec(memory_space=pltpu.SMEM)] + [spec] * len(args),
        out_specs=[spec] * len(outs),
        compiler_params=pltpu.CompilerParams(vmem_limit_bytes=VMEM_LIMIT),
    )(where, *args)


def project_kernel(where_ref, own, nxt, opp_a, opp_b, prev, w_mine, w_theirs, out_ref):
    zh, c = where_ref[0], where_ref[3]
    acc = [jnp.zeros((own.shape[0], 2 * DH), F32)] * 2
    for dz in range(4):
        block = pl.ds(pl.multiple_of(lax.rem(zh + dz, 4) * 1024, 1024), 1024)
        if dz == 2:
            rows = jnp.concatenate([opp_a[...], opp_b[...]], 0)
        else:
            rows = (own, nxt, None, prev)[dz][...]
        for j, w in enumerate((w_mine, w_theirs)):
            acc[j] = acc[j] + jnp.dot(rows, w[block], preferred_element_type=F32)
    shape = (out_ref.shape[0],) + out_ref.shape[2:]
    out_ref[:, c] = acc[0].astype(BF).reshape(shape)
    out_ref[:, 1 - c] = acc[1].astype(BF).reshape(shape)


def project(where, pieces, weights):
    out = jax.ShapeDtypeStruct((8, 2, pieces[0].shape[0] // 8, 2 * DH), BF)
    return kernel_call(project_kernel, [out], where, *pieces, *weights)[0]


def attend_kernel(chunk, last, where_ref, q_ref, kv_ref, *refs):
    length, base = where_ref[0], where_ref[1]
    rows = kv_ref.shape[0]
    per = rows // 16
    if last:
        acc_in, stats_in, outs = refs[0], refs[1], refs[2:]
    else:
        acc_out, stats_out = refs
    row = lax.broadcasted_iota(jnp.int32, (rows, 128), 0)
    shift = per.bit_length() - 1
    position = (row >> (shift + 1)) * 512 + base + ((row >> shift) & 1) * 64 + chunk * per + (row & (per - 1))
    bias = jnp.where(position < length, 0.0, -1e30)
    bias = jnp.concatenate([bias, bias], axis=1)
    keys = kv_ref[:, :DH]
    values = kv_ref[:, DH:].T
    for i in range(8):
        group = where_ref[2 + i // 2] * 2 + i % 2
        q = q_ref[pl.ds(pl.multiple_of(group * 256, 256), 256)]
        s = lax.dot_general(keys, q, (((1,), (1,)), ((), ())), preferred_element_type=F32) + bias
        high = jnp.max(s, axis=0, keepdims=True)
        if last:
            before = stats_in[i, 0:1]
            high = jnp.maximum(high, before)
        p = jnp.exp2((s - high) * EXP_SCALE)
        total = jnp.sum(p, axis=0, keepdims=True)
        acc = jnp.dot(values, p.astype(BF), preferred_element_type=F32)
        if not last:
            acc_out[i] = acc
            stats_out[i] = jnp.concatenate([high, total, jnp.zeros((6, 256), F32)], 0)
            continue
        keep = jnp.exp2((before - high) * EXP_SCALE)
        total = total + stats_in[i, 1:2] * keep
        acc = acc + acc_in[i] * keep
        lse = high * EXP_SCALE + jnp.log2(total)
        first = lse.astype(BF).astype(F32)
        second = (lse - first).astype(BF).astype(F32)
        stats = jnp.concatenate([first, second, lse - first - second, jnp.zeros((13, 256), F32)], 0)
        outs[i // 2][i % 2, :DH] = (acc * (1.0 / total)).astype(BF)
        outs[i // 2][i % 2, DH:] = stats.astype(BF)


def attend(where, q, kv, chunk, before=None):
    last = before is not None
    if last:
        outs = [jax.ShapeDtypeStruct((2, DH + 16, 256), BF)] * 4
    else:
        outs = [jax.ShapeDtypeStruct((8, DH, 256), F32), jax.ShapeDtypeStruct((8, 8, 256), F32)]
    kernel = functools.partial(attend_kernel, chunk, last)
    return kernel_call(kernel, outs, where, q, kv, *(before or ()))


def merge_kernel(where_ref, a_ref, b_ref, c_ref, d_ref, *outs):
    zh = where_ref[0]
    refs = (a_ref, b_ref, c_ref, d_ref)
    contexts = []
    for side in range(2):
        stats = [ref[side, DH:].astype(F32) for ref in refs]
        lse = [s[0:1] + s[1:2] + s[2:3] for s in stats]
        high = functools.reduce(jnp.maximum, lse)
        weight = [jnp.exp2(v - high) for v in lse]
        inverse = 1.0 / sum(weight)
        context = sum(ref[side, :DH].astype(F32) * (w * inverse) for ref, w in zip(refs, weight))
        contexts.append(context.T.astype(BF))
    for d in range(4):
        for m in range(4):

            @pl.when(lax.rem(zh + d, 4) == m)
            def _(d=d, m=m):
                for side in range(2):
                    outs[d][side * 64 : (side + 1) * 64] = contexts[side][m * 64 : (m + 1) * 64]


def merge(where, parts):
    return kernel_call(merge_kernel, [jax.ShapeDtypeStruct((128, DH), BF)] * 4, where, *parts)


def output_kernel(where_ref, *refs):
    c = where_ref[3]
    w_ref, out_mine, out_theirs = refs[4:]
    rows = jnp.concatenate([ref[...] for ref in refs[:4]], 1)
    for i in range(8):
        cols = slice(i * 512, (i + 1) * 512)
        acc = jnp.dot(rows, w_ref[:, cols], preferred_element_type=F32)
        low, high = acc[:64], acc[64:]
        out_mine[:, cols] = jnp.where(c == 0, low, high)
        out_theirs[:, cols] = jnp.where(c == 0, high, low)


def output(where, ctx, w):
    return kernel_call(output_kernel, [jax.ShapeDtypeStruct((64, 4096), F32)] * 2, where, *ctx, w)


def finish_kernel(where_ref, mine, other, residual, gain, hidden, normed):
    x = residual[...].astype(F32) + (mine[...] + other[...])
    scale = lax.rsqrt(jnp.mean(x * x, -1, keepdims=True) + 1e-06)
    hidden[...] = x.astype(BF)
    normed[...] = (x * scale * gain[...]).astype(BF)


def finish(where, *args):
    return kernel_call(finish_kernel, [jax.ShapeDtypeStruct(args[2].shape, BF)] * 2, where, *args)


def shards(memory, kv_weight, mem_lengths, queries, out_weight, residual, norm_gain):
    zh, x, yh, yl, zl, c = (lax.axis_index(a) for a in (Z, X, "yh", "yl", "zl", "c"))
    y = yh * 2 + yl
    where = jnp.stack([zh, x, y, c]).astype(jnp.int32)

    mine = pick(kv_weight[:, :512], kv_weight[:, 512:], c)
    theirs = pick(kv_weight[:, 512:], kv_weight[:, :512], c)
    w_c = swap(theirs, "c")
    w_z = swap(mine, "zl")
    w_zc = lax.ppermute(theirs, ("zl", "c"), [(i, 3 - i) for i in range(4)])
    rows = pair(pair(mine, w_c, c), pair(w_z, w_zc, c), zl)
    w_mine = lax.all_gather(rows, XY, axis=0, tiled=True)

    step = memory.shape[1] // CHUNKS
    half = 4 * step
    chunks = []
    for j in range(CHUNKS):
        own = memory[:, j * step : (j + 1) * step].reshape(8 * step, 1024)
        prev = lax.ppermute(own, Z, FWD)
        nxt = lax.ppermute(own, Z, BWD)
        opp_a = lax.ppermute(prev[:half], Z, FWD)
        opp_b = lax.ppermute(nxt[half:], Z, BWD)
        chunks.append([own, nxt, opp_a, opp_b, prev])

    ow = lax.dynamic_slice(out_weight, (c * DH, (x * 4 + y) * 256), (DH, 256))
    ow = [ow] + [lax.ppermute(ow, Z, [(i, (i + 4 - d) % 4) for i in range(4)]) for d in (1, 2, 3)]
    ow = jnp.concatenate(ow, 0)

    w_mine, ow = lax.optimization_barrier((w_mine, ow))
    ow = lax.all_gather(ow, XY, axis=1, tiled=True)
    w_theirs = swap(w_mine, "c")

    other = pick(queries[:, DH:], queries[:, :DH], c)
    other = swap(other, "c")
    q = pair(pick(queries[:, :DH], queries[:, DH:], c), other, c)
    other = swap(q, "zl")
    q = pair(q, other, zl)
    q = pair(q, swap(q, "yl"), yl)

    length = lax.dynamic_index_in_dim(mem_lengths, x * 2 + yh, 0, keepdims=False)
    here = yl * 2 + zl
    here = jnp.stack([length, yl * 256 + zl * 128, here, here ^ 1, here ^ 2, here ^ 3]).astype(jnp.int32)
    state = None
    for j, pieces in enumerate(chunks):
        both = project(where, pieces, (w_mine, w_theirs))
        both = lax.all_to_all(both.reshape(16, step, 512), (X, "yh", "c"), 0, 0, tiled=True)
        state = attend(here, q, both.reshape(16 * step, 512), j, state)

    own, to_zl, to_yl, to_both = state
    parts = (
        own,
        swap(to_zl, "zl"),
        swap(to_yl, "yl"),
        lax.ppermute(to_both, ("yl", "zl"), [(i, 3 - i) for i in range(4)]),
    )
    pieces = merge(where, parts)
    ctx = [pieces[0]] + [lax.ppermute(pieces[4 - d], Z, [(i, (i + 4 - d) % 4) for i in range(4)]) for d in (1, 2, 3)]
    mine, theirs = output(where, ctx, ow)
    return tuple(finish(where, mine, swap(theirs, "c"), residual, norm_gain.reshape(1, -1)))


def solution(mesh):
    fine = Mesh(mesh.devices.reshape(4, 4, 2, 2, 2, 2), (Z, X, "yh", "yl", "zl", "c"))
    seq = (X, "yh", "yl", "zl", "c")
    in_specs = (
        P(None, seq, Z),
        P(seq, Z),
        P(),
        P(seq, Z),
        P(Z, None),
        P(seq + (Z,), None),
        P(),
    )
    out_specs = (P(seq + (Z,), None), P(seq + (Z,), None))
    return jax.shard_map(shards, mesh=fine, in_specs=in_specs, out_specs=out_specs, check_vma=False)
```

time: 272 us -> 254 us (0.934)
  Pallas kernels: 47.4 us -> 21.4 us
  local copies, waits for them, and re-layouts: 7.5 us -> 12.1 us
  waiting for transfers between devices: 134 us -> 137 us
    pallas_call x7, Pallas kernels: 47.4 us -> 21.4 us  [kernel_call(): pl.pallas_call(kernel, out_shape=outs, in_specs=[pl.BlockSpec(memory_spac...]
    unnamed x40 -> x20, local copies, waits for them, and re-layouts: 3.88 us -> 8.88 us
    all_to_all x2, waiting for transfers between devices: 0.01 us -> 4.74 us  [shards(): lax.all_to_all(both.reshape(16, step, 512), (X, 'yh', 'c'), 0, 0, tiled=T...]
  transfers between devices with their start and end apart: 29 -> 29, of which waited for: 16 -> 17; matrix products, arithmetic and copies ran while one was open for 3% -> 3% of each run, Pallas kernels for 13% -> 7%
where the time goes in v2:
time: 254 us
  waiting for transfers between devices  137 us (54%)
  starting transfers between devices  62.5 us (25%)
  Pallas kernels  21.4 us (8%)
  between operations  14.2 us (6%)
  local copies, waits for them, and re-layouts  12.1 us (5%)
  other arithmetic  6.33 us (2%)
    all_gather x1, waiting for transfers between devices, shards(): w_mine = lax.all_gather(rows, XY, axis=0, tiled=True)  36.8 us
    ppermute x2, waiting for transfers between devices, shards(): opp_b = lax.ppermute(nxt[half:], Z, BWD)  29.6 us
    pallas_call x7, Pallas kernels, kernel_call(): pl.pallas_call(kernel, out_shape=outs, in_specs=[pl.BlockSpec(memory_spac...  21.4 us
    ppermute x2, waiting for transfers between devices, shards(): prev = lax.ppermute(own, Z, FWD)  19.5 us
    ppermute x2, waiting for transfers between devices, shards(): opp_a = lax.ppermute(prev[:half], Z, FWD)  14.4 us
    ppermute x9, starting transfers between devices, swap(): return lax.ppermute(a, axis, [(0, 1), (1, 0)])  13.6 us
    all_to_all x2, starting transfers between devices, shards(): lax.all_to_all(both.reshape(16, step, 512), (X, 'yh', 'c'), 0, 0, tiled=T...  13.5 us
    ppermute x3, waiting for transfers between devices, shards(): lax.ppermute(ow, Z, [(i, (i + 4 - d) % 4) for i in range(4)])  10.5 us
  transfers between devices with their start and end apart: 29, of which 17 were waited for; matrix products, arithmetic and copies ran while one was open for 3% of the time, Pallas kernels for 7%

profile of v2, /device:TPU:1, one launch (start us, length us, event | category | flops | bytes accessed | tf_op | source)
XLA Modules:
  0.0 253.7 jit_solution(16473290260435661705)
XLA Ops:
  7.2 1.0 broadcast_select_fusion.3
  8.2 3.3 %collective-permute-start.7 = (bf16[64,512]{1,0:T(8,128)(2,1)S(1)}, bf16[64,512]{1,0:T(8,128)(2,1)S(1)}, u32[]{:S(2)}, u32[]{:S(2)}) collective-permute-start(bf16[64,512]{1,0:T(8,128)(2,1)S(1)} %get-tuple-element.35), channel_id=1, source_target_pairs={{0,1},{1,0},{2,3},{3,2},{4,5},{5,4},{6,7},{7,6},{8,9},{9,8},{10,11... | collective-permute-start | bytes 196616 | tf_op jit(solution)/shard_map/ppermute | solution.py:26
  11.5 1.4 collective-permute-start.8
  13.0 2.9 %collective-permute-done.9 = bf16[64,512]{1,0:T(8,128)(2,1)S(1)} collective-permute-done((bf16[64,512]{1,0:T(8,128)(2,1)S(1)}, bf16[64,512]{1,0:T(8,128)(2,1)S(1)}, u32[]{:S(2)}, u32[]{:S(2)}) %collective-permute-start.9) | collective-permute-done | bytes 65568 | tf_op jit(solution)/shard_map/ppermute | solution.py:182
  18.2 1.2 collective-permute-start.12
  19.4 5.3 %collective-permute-start.11 = (bf16[256,256]{1,0:T(8,128)(2,1)S(1)}, bf16[256,256]{1,0:T(8,128)(2,1)S(1)}, u32[]{:S(2)}, u32[]{:S(2)}) collective-permute-start(bf16[256,256]{1,0:T(8,128)(2,1)S(1)} %dynamic_slice.8), channel_id=1, source_target_pairs={{0,128},{64,192},{128,0},{192,64},{1,129},{65,193},{129,1},{193,65... | collective-permute-start | bytes 393224 | tf_op jit(solution)/shard_map/ppermute | solution.py:198
  24.7 2.4 collective-permute-start.10
  27.1 5.4 %collective-permute-done.11 = bf16[256,256]{1,0:T(8,128)(2,1)S(1)} collective-permute-done((bf16[256,256]{1,0:T(8,128)(2,1)S(1)}, bf16[256,256]{1,0:T(8,128)(2,1)S(1)}, u32[]{:S(2)}, u32[]{:S(2)}) %collective-permute-start.11) | collective-permute-done | bytes 131104 | tf_op jit(solution)/shard_map/ppermute | solution.py:198
  32.4 5.2 %collective-permute-done.10 = bf16[256,256]{1,0:T(8,128)(2,1)S(1)} collective-permute-done((bf16[256,256]{1,0:T(8,128)(2,1)S(1)}, bf16[256,256]{1,0:T(8,128)(2,1)S(1)}, u32[]{:S(2)}, u32[]{:S(2)}) %collective-permute-start.10) | collective-permute-done | bytes 131104 | tf_op jit(solution)/shard_map/ppermute | solution.py:198
  38.4 36.8 %all-gather.3.cloned.1.call-done.w_mine = bf16[4096,512]{1,0:T(8,128)(2,1)} async-done(((bf16[256,512]{1,0:T(8,128)(2,1)}), bf16[4096,512]{1,0:T(8,128)(2,1)}) %all-gather.3.cloned.1.call-update) | async-done | bytes 4194320 | tf_op jit(solution)/shard_map/all_gather | solution.py:184
  75.2 0.9 collective-permute-start.13
  76.2 2.3 collective-permute-start.15
  78.6 1.7 collective-permute-start.14
  80.3 19.5 %collective-permute-done.15.prev = bf16[256,1024]{1,0:T(8,128)(2,1)S(1)} collective-permute-done((bf16[256,1024]{1,0:T(8,128)(2,1)S(1)}, bf16[256,1024]{1,0:T(8,128)(2,1)S(1)}, u32[]{:S(2)}, u32[]{:S(2)}) %collective-permute-start.15) | collective-permute-done | bytes 524320 | tf_op jit(solution)/shard_map/ppermute | solution.py:191
  99.8 4.8 %collective-permute-start.16 = (bf16[128,1024]{1,0:T(8,128)(2,1)S(1)}, bf16[128,1024]{1,0:T(8,128)(2,1)S(1)}, u32[]{:S(2)}, u32[]{:S(2)}) collective-permute-start(bf16[128,1024]{1,0:T(8,128)(2,1)S(1)} %slice.46), channel_id=1, source_target_pairs={{0,64},{64,128},{128,192},{192,0},{1,65},{65,129},{129,193},{193,1... | collective-permute-start | bytes 786440 | tf_op jit(solution)/shard_map/ppermute | solution.py:193
  104.6 1.3 collective-permute-start
  105.9 4.3 %collective-permute-start.4 = (bf16[256,1024]{1,0:T(8,128)(2,1)S(1)}, bf16[256,1024]{1,0:T(8,128)(2,1)S(1)}, u32[]{:S(2)}, u32[]{:S(2)}) collective-permute-start(bf16[256,1024]{1,0:T(8,128)(2,1)S(1)} %bitcast.17), channel_id=1, source_target_pairs={{0,64},{64,128},{128,192},{192,0},{1,65},{65,129},{129,193},{193,1... | collective-permute-start | bytes 1572872 | tf_op jit(solution)/shard_map/ppermute | solution.py:191
  111.7 3.7 %collective-permute-done.16.opp_a = bf16[128,1024]{1,0:T(8,128)(2,1)S(1)} collective-permute-done((bf16[128,1024]{1,0:T(8,128)(2,1)S(1)}, bf16[128,1024]{1,0:T(8,128)(2,1)S(1)}, u32[]{:S(2)}, u32[]{:S(2)}) %collective-permute-start.16) | collective-permute-done | bytes 262176 | tf_op jit(solution)/shard_map/ppermute | solution.py:193
  115.5 1.8 collective-permute-start.1
  117.3 27.1 %collective-permute-done.17.opp_b = bf16[128,1024]{1,0:T(8,128)(2,1)} collective-permute-done((bf16[128,1024]{1,0:T(8,128)(2,1)}, bf16[128,1024]{1,0:T(8,128)(2,1)}, u32[]{:S(2)}, u32[]{:S(2)}) %collective-permute-start.17) | collective-permute-done | bytes 262176 | tf_op jit(solution)/shard_map/ppermute | solution.py:194
  144.4 2.2 copy-done
  146.7 5.6 %shard_map.87 = bf16[8,2,32,512]{3,2,1,0:T(8,128)(2,1)} custom-call(s32[4]{0:T(128)S(1)} %pad_add_fusion.where_ref, bf16[256,1024]{1,0:T(8,128)(2,1)S(1)} %bitcast.22, bf16[256,1024]{1,0:T(8,128)(2,1)S(1)} %collective-permute-done.14.nxt, bf16[128,1024]{1,0:T(8,128)(2,1)S(1)} %collective-permute-done.16.opp_a, ...), custom_call_target="tpu_custom_call" | custom-call | tf_op jit(solution)/shard_map/pallas_call | solution.py:40
  152.3 5.5 %all-to-all-start.1 = ((bf16[16,32,512]{2,1,0:T(8,128)(2,1)}), bf16[16,32,512]{2,1,0:T(8,128)(2,1)S(1)}, u32[]{:S(2)}, u32[]{:S(2)}) async-start(bf16[16,32,512]{2,1,0:T(8,128)(2,1)} %bitcast.13), calls=%async_computation.1 | async-start | bytes 1048576 | tf_op jit(solution)/shard_map/all_to_all | solution.py:218
  157.8 1.4 maximum_select_fusion.1
  159.5 4.5 %collective-permute-start.5 = (bf16[128,1024]{1,0:T(8,128)(2,1)S(1)}, bf16[128,1024]{1,0:T(8,128)(2,1)S(1)}, u32[]{:S(2)}, u32[]{:S(2)}) collective-permute-start(bf16[128,1024]{1,0:T(8,128)(2,1)S(1)} %slice.44), channel_id=1, source_target_pairs={{0,64},{64,128},{128,192},{192,0},{1,65},{65,129},{129,193},{193,1... | collective-permute-start | bytes 786440 | tf_op jit(solution)/shard_map/ppermute | solution.py:193
  164.2 10.7 %collective-permute-done.5.opp_a = bf16[128,1024]{1,0:T(8,128)(2,1)S(1)} collective-permute-done((bf16[128,1024]{1,0:T(8,128)(2,1)S(1)}, bf16[128,1024]{1,0:T(8,128)(2,1)S(1)}, u32[]{:S(2)}, u32[]{:S(2)}) %collective-permute-start.5) | collective-permute-done | bytes 262176 | tf_op jit(solution)/shard_map/ppermute | solution.py:193
  174.8 2.5 collective-permute-done.6.opp_b
  177.3 2.2 copy-done.1
  179.5 5.3 %shard_map.86 = bf16[8,2,32,512]{3,2,1,0:T(8,128)(2,1)} custom-call(s32[4]{0:T(128)S(1)} %pad_add_fusion.where_ref, bf16[256,1024]{1,0:T(8,128)(2,1)S(1)} %bitcast.18, bf16[256,1024]{1,0:T(8,128)(2,1)S(1)} %collective-permute-done.3.nxt, bf16[128,1024]{1,0:T(8,128)(2,1)S(1)} %collective-permute-done.5.opp_a, ...), custom_call_target="tpu_custom_call" | custom-call | tf_op jit(solution)/shard_map/pallas_call | solution.py:40
  184.8 7.9 %all-to-all-start = ((bf16[16,32,512]{2,1,0:T(8,128)(2,1)}), bf16[16,32,512]{2,1,0:T(8,128)(2,1)}, u32[]{:S(2)}, u32[]{:S(2)}) async-start(bf16[16,32,512]{2,1,0:T(8,128)(2,1)} %bitcast.10), calls=%async_computation | async-start | bytes 1048576 | tf_op jit(solution)/shard_map/all_to_all | solution.py:218
  194.2 1.4 maximum_select_fusion.q_ref
  195.7 1.0 copy-done.4
  196.7 2.6 %shard_map.88 = (f32[8,256,256]{2,1,0:T(8,128)S(1)}, f32[8,8,256]{2,1,0:T(8,128)S(1)}) custom-call(s32[6]{0:T(128)S(1)} %stack.44.where_ref, bf16[2048,256]{1,0:T(8,128)(2,1)S(1)} %maximum_select_fusion.q_ref, bf16[512,512]{1,0:T(8,128)(2,1)S(1)} %bitcast.19), custom_call_target="tpu_custom_call" | custom-call | tf_op jit(solution)/shard_map/pallas_call | solution.py:40
  199.3 4.7 %all-to-all-done = bf16[16,32,512]{2,1,0:T(8,128)(2,1)} async-done(((bf16[16,32,512]{2,1,0:T(8,128)(2,1)}), bf16[16,32,512]{2,1,0:T(8,128)(2,1)}, u32[]{:S(2)}, u32[]{:S(2)}) %all-to-all-start) | async-done | bytes 524320 | tf_op jit(solution)/shard_map/all_to_all | solution.py:218
  204.1 3.3 %shard_map.89 = (bf16[2,272,256]{2,1,0:T(8,128)(2,1)S(1)}, bf16[2,272,256]{2,1,0:T(8,128)(2,1)S(1)}, bf16[2,272,256]{2,1,0:T(8,128)(2,1)S(1)}, bf16[2,272,256]{2,1,0:T(8,128)(2,1)S(1)}) custom-call(s32[6]{0:T(128)S(1)} %stack.44.where_ref, bf16[2048,256]{1,0:T(8,128)(2,1)S(1)} %maximum_select_fusion.q_ref, bf16[512,512]{1,0:T(8,128)(2,1)} %bitcast.11.kv_ref, ...), custom_call_target="tpu_custom_call" | custom-call | tf_op jit(solution)/shard_map/pallas_call | solution.py:40
  207.6 2.5 collective-permute-start.20
  210.1 4.3 %collective-permute-done.18.b_ref = bf16[2,272,256]{2,1,0:T(8,128)(2,1)S(1)} collective-permute-done((bf16[2,272,256]{2,1,0:T(8,128)(2,1)S(1)}, bf16[2,272,256]{2,1,0:T(8,128)(2,1)S(1)}, u32[]{:S(2)}, u32[]{:S(2)}) %collective-permute-start.18) | collective-permute-done | bytes 278560 | tf_op jit(solution)/shard_map/ppermute | solution.py:26
  214.9 5.4 %collective-permute-done.20.d_ref = bf16[2,272,256]{2,1,0:T(8,128)(2,1)S(1)} collective-permute-done((bf16[2,272,256]{2,1,0:T(8,128)(2,1)S(1)}, bf16[2,272,256]{2,1,0:T(8,128)(2,1)S(1)}, u32[]{:S(2)}, u32[]{:S(2)}) %collective-permute-start.20) | collective-permute-done | bytes 278560 | tf_op jit(solution)/shard_map/ppermute | solution.py:226
  220.3 1.0 shard_map.90
  221.2 2.6 %collective-permute-start.21 = (bf16[128,256]{1,0:T(8,128)(2,1)S(1)}, bf16[128,256]{1,0:T(8,128)(2,1)S(1)}, u32[]{:S(2)}, u32[]{:S(2)}) collective-permute-start(bf16[128,256]{1,0:T(8,128)(2,1)S(1)} %get-tuple-element.24), channel_id=1, source_target_pairs={{0,192},{64,0},{128,64},{192,128},{1,193},{65,1},{129,65},{193,129... | collective-permute-start | bytes 196616 | tf_op jit(solution)/shard_map/ppermute | solution.py:229
  223.8 3.7 %collective-permute-start.22 = (bf16[128,256]{1,0:T(8,128)(2,1)S(1)}, bf16[128,256]{1,0:T(8,128)(2,1)S(1)}, u32[]{:S(2)}, u32[]{:S(2)}) collective-permute-start(bf16[128,256]{1,0:T(8,128)(2,1)S(1)} %get-tuple-element.25), channel_id=1, source_target_pairs={{0,128},{64,192},{128,0},{192,64},{1,129},{65,193},{129,1},{193,65... | collective-permute-start | bytes 196616 | tf_op jit(solution)/shard_map/ppermute | solution.py:229
  227.5 4.0 %collective-permute-done.22.refs_2_ = bf16[128,256]{1,0:T(8,128)(2,1)S(1)} collective-permute-done((bf16[128,256]{1,0:T(8,128)(2,1)S(1)}, bf16[128,256]{1,0:T(8,128)(2,1)S(1)}, u32[]{:S(2)}, u32[]{:S(2)}) %collective-permute-start.22) | collective-permute-done | bytes 65568 | tf_op jit(solution)/shard_map/ppermute | solution.py:229
  231.5 1.7 collective-permute-done.23.refs_3_
  233.3 3.4 %copy-done.2 = bf16[1024,4096]{1,0:T(8,128)(2,1)S(1)} copy-done((bf16[1024,4096]{1,0:T(8,128)(2,1)S(1)}, bf16[1024,4096]{1,0:T(8,128)(2,1)}, u32[]{:S(2)}) %copy-start.2) | copy-done | bytes 8388632
  236.6 1.8 shard_map.91
  238.5 4.3 %collective-permute-start.24 = (f32[64,4096]{1,0:T(8,128)S(1)}, f32[64,4096]{1,0:T(8,128)S(1)}, u32[]{:S(2)}, u32[]{:S(2)}) collective-permute-start(f32[64,4096]{1,0:T(8,128)S(1)} %get-tuple-element.29), channel_id=1, source_target_pairs={{0,1},{1,0},{2,3},{3,2},{4,5},{5,4},{6,7},{7,6},{8,9},{9,8},{10,11... | collective-permute-start | bytes 3145736 | tf_op jit(solution)/shard_map/ppermute | solution.py:26
  242.8 2.3 collective-permute-done.24.other
  245.0 1.8 shard_map.92
  (57 shorter events, 7.5 us)
Async XLA Ops:
  7.2 69.0 %copy-start.7 = (bf16[8,64,1024]{2,1,0:T(8,128)(2,1)S(1)}, bf16[8,64,1024]{2,1,0:T(8,128)(2,1)}, u32[]{:S(2)}) copy-start(bf16[8,64,1024]{2,1,0:T(8,128)(2,1)} %param.7) | copy-start | bytes 3145732
  7.2 68.0 %all-gather.3.cloned.1.call-start = ((), (), s32[]{:S(2)}) async-start(), calls=%async_computation.2 | async-start | bytes 4456448 | tf_op jit(solution)/shard_map/all_gather | solution.py:184
  8.2 4.7 %collective-permute-start.7 = (bf16[64,512]{1,0:T(8,128)(2,1)S(1)}, bf16[64,512]{1,0:T(8,128)(2,1)S(1)}, u32[]{:S(2)}, u32[]{:S(2)}) collective-permute-start(bf16[64,512]{1,0:T(8,128)(2,1)S(1)} %get-tuple-element.35), channel_id=1, source_target_pairs={{0,1},{1,0},{2,3},{3,2},{4,5},{5,4},{6,7},{7,6},{8,9},{9,8},{10,11... | collective-permute-start | bytes 196616 | tf_op jit(solution)/shard_map/ppermute | solution.py:26
  11.5 4.4 %collective-permute-start.9 = (bf16[64,512]{1,0:T(8,128)(2,1)S(1)}, bf16[64,512]{1,0:T(8,128)(2,1)S(1)}, u32[]{:S(2)}, u32[]{:S(2)}) collective-permute-start(bf16[64,512]{1,0:T(8,128)(2,1)S(1)} %get-tuple-element.35), channel_id=1, source_target_pairs={{0,3},{1,2},{2,1},{3,0},{4,7},{5,6},{6,5},{7,4},{8,11},{9,10},{10,... | collective-permute-start | bytes 196616 | tf_op jit(solution)/shard_map/ppermute | solution.py:182
  11.5 4.9 %collective-permute-start.8 = (bf16[64,512]{1,0:T(8,128)(2,1)S(1)}, bf16[64,512]{1,0:T(8,128)(2,1)S(1)}, u32[]{:S(2)}, u32[]{:S(2)}) collective-permute-start(bf16[64,512]{1,0:T(8,128)(2,1)S(1)} %get-tuple-element.34), channel_id=1, source_target_pairs={{0,2},{2,0},{1,3},{3,1},{4,6},{6,4},{5,7},{7,5},{8,10},{10,8},{9,1... | collective-permute-start | bytes 196616 | tf_op jit(solution)/shard_map/ppermute | solution.py:26
  17.2 216.0 %all-gather.5.cloned.1.call-start = ((), (), s32[]{:S(2)}) async-start(), calls=%async_computation.3 | async-start | bytes 8912896 | tf_op jit(solution)/shard_map/all_gather | solution.py:202
  18.2 86.4 %copy-start.8 = (bf16[256,512]{1,0:T(8,128)(2,1)S(1)}, bf16[256,512]{1,0:T(8,128)(2,1)}, u32[]{:S(2)}) copy-start(bf16[256,512]{1,0:T(8,128)(2,1)} %param.10) | copy-start | bytes 786436
  18.2 8.9 %collective-permute-start.12 = (bf16[256,256]{1,0:T(8,128)(2,1)S(1)}, bf16[256,256]{1,0:T(8,128)(2,1)S(1)}, u32[]{:S(2)}, u32[]{:S(2)}) collective-permute-start(bf16[256,256]{1,0:T(8,128)(2,1)S(1)} %dynamic_slice.8), channel_id=1, source_target_pairs={{0,64},{64,128},{128,192},{192,0},{1,65},{65,129},{129,193},{193,1... | collective-permute-start | bytes 393224 | tf_op jit(solution)/shard_map/ppermute | solution.py:198
  19.4 13.0 %collective-permute-start.11 = (bf16[256,256]{1,0:T(8,128)(2,1)S(1)}, bf16[256,256]{1,0:T(8,128)(2,1)S(1)}, u32[]{:S(2)}, u32[]{:S(2)}) collective-permute-start(bf16[256,256]{1,0:T(8,128)(2,1)S(1)} %dynamic_slice.8), channel_id=1, source_target_pairs={{0,128},{64,192},{128,0},{192,64},{1,129},{65,193},{129,1},{193,65... | collective-permute-start | bytes 393224 | tf_op jit(solution)/shard_map/ppermute | solution.py:198
  24.7 12.9 %collective-permute-start.10 = (bf16[256,256]{1,0:T(8,128)(2,1)S(1)}, bf16[256,256]{1,0:T(8,128)(2,1)S(1)}, u32[]{:S(2)}, u32[]{:S(2)}) collective-permute-start(bf16[256,256]{1,0:T(8,128)(2,1)S(1)} %dynamic_slice.8), channel_id=1, source_target_pairs={{0,192},{64,0},{128,64},{192,128},{1,193},{65,1},{129,65},{193,129... | collective-permute-start | bytes 393224 | tf_op jit(solution)/shard_map/ppermute | solution.py:198
  75.2 69.2 %collective-permute-start.13 = (bf16[4096,512]{1,0:T(8,128)(2,1)}, bf16[4096,512]{1,0:T(8,128)(2,1)}, u32[]{:S(2)}, u32[]{:S(2)}) collective-permute-start(bf16[4096,512]{1,0:T(8,128)(2,1)} %all-gather.3.cloned.1.call-done.w_mine), channel_id=1, source_target_pairs={{0,1},{1,0},{2,3},{3,2},{4,5},{5,4},{6,7},{7,6},{8,9},{9,8},{10,11... | collective-permute-start | bytes 12582920 | tf_op jit(solution)/shard_map/ppermute | solution.py:26
  76.2 23.5 %collective-permute-start.15 = (bf16[256,1024]{1,0:T(8,128)(2,1)S(1)}, bf16[256,1024]{1,0:T(8,128)(2,1)S(1)}, u32[]{:S(2)}, u32[]{:S(2)}) collective-permute-start(bf16[256,1024]{1,0:T(8,128)(2,1)S(1)} %bitcast.20), channel_id=1, source_target_pairs={{0,64},{64,128},{128,192},{192,0},{1,65},{65,129},{129,193},{193,1... | collective-permute-start | bytes 1572872 | tf_op jit(solution)/shard_map/ppermute | solution.py:191
  78.6 27.3 %collective-permute-start.14 = (bf16[256,1024]{1,0:T(8,128)(2,1)S(1)}, bf16[256,1024]{1,0:T(8,128)(2,1)S(1)}, u32[]{:S(2)}, u32[]{:S(2)}) collective-permute-start(bf16[256,1024]{1,0:T(8,128)(2,1)S(1)} %bitcast.21), channel_id=1, source_target_pairs={{0,192},{64,0},{128,64},{192,128},{1,193},{65,1},{129,65},{193,129... | collective-permute-start | bytes 1572872 | tf_op jit(solution)/shard_map/ppermute | solution.py:192
  99.8 15.7 %collective-permute-start.16 = (bf16[128,1024]{1,0:T(8,128)(2,1)S(1)}, bf16[128,1024]{1,0:T(8,128)(2,1)S(1)}, u32[]{:S(2)}, u32[]{:S(2)}) collective-permute-start(bf16[128,1024]{1,0:T(8,128)(2,1)S(1)} %slice.46), channel_id=1, source_target_pairs={{0,64},{64,128},{128,192},{192,0},{1,65},{65,129},{129,193},{193,1... | collective-permute-start | bytes 786440 | tf_op jit(solution)/shard_map/ppermute | solution.py:193
  104.6 6.3 %collective-permute-start = (bf16[256,256]{1,0:T(8,128)(2,1)S(1)}, bf16[256,256]{1,0:T(8,128)(2,1)S(1)}, u32[]{:S(2)}, u32[]{:S(2)}) collective-permute-start(bf16[256,256]{1,0:T(8,128)(2,1)S(1)} %get-tuple-element.33), channel_id=1, source_target_pairs={{0,1},{1,0},{2,3},{3,2},{4,5},{5,4},{6,7},{7,6},{8,9},{9,8},{10,11... | collective-permute-start | bytes 393224 | tf_op jit(solution)/shard_map/ppermute | solution.py:26
  105.9 58.2 %collective-permute-start.3 = (bf16[256,1024]{1,0:T(8,128)(2,1)S(1)}, bf16[256,1024]{1,0:T(8,128)(2,1)S(1)}, u32[]{:S(2)}, u32[]{:S(2)}) collective-permute-start(bf16[256,1024]{1,0:T(8,128)(2,1)S(1)} %bitcast.16), channel_id=1, source_target_pairs={{0,192},{64,0},{128,64},{192,128},{1,193},{65,1},{129,65},{193,129... | collective-permute-start | bytes 1572872 | tf_op jit(solution)/shard_map/ppermute | solution.py:192
  105.9 53.6 %collective-permute-start.4 = (bf16[256,1024]{1,0:T(8,128)(2,1)S(1)}, bf16[256,1024]{1,0:T(8,128)(2,1)S(1)}, u32[]{:S(2)}, u32[]{:S(2)}) collective-permute-start(bf16[256,1024]{1,0:T(8,128)(2,1)S(1)} %bitcast.17), channel_id=1, source_target_pairs={{0,64},{64,128},{128,192},{192,0},{1,65},{65,129},{129,193},{193,1... | collective-permute-start | bytes 1572872 | tf_op jit(solution)/shard_map/ppermute | solution.py:191
  110.9 33.5 %collective-permute-start.17 = (bf16[128,1024]{1,0:T(8,128)(2,1)}, bf16[128,1024]{1,0:T(8,128)(2,1)}, u32[]{:S(2)}, u32[]{:S(2)}) collective-permute-start(bf16[128,1024]{1,0:T(8,128)(2,1)} %slice.47), channel_id=1, source_target_pairs={{0,192},{64,0},{128,64},{192,128},{1,193},{65,1},{129,65},{193,129... | collective-permute-start | bytes 786440 | tf_op jit(solution)/shard_map/ppermute | solution.py:194
  115.5 42.4 %collective-permute-start.1 = (bf16[512,256]{1,0:T(8,128)(2,1)}, bf16[512,256]{1,0:T(8,128)(2,1)}, u32[]{:S(2)}, u32[]{:S(2)}) collective-permute-start(bf16[512,256]{1,0:T(8,128)(2,1)} %maximum_select_fusion.2), channel_id=1, source_target_pairs={{0,2},{2,0},{1,3},{3,1},{4,6},{6,4},{5,7},{7,5},{8,10},{10,8},{9,1... | collective-permute-start | bytes 786440 | tf_op jit(solution)/shard_map/ppermute | solution.py:26
  144.4 2.2 copy-start
  152.3 32.6 %all-to-all-start.1 = ((bf16[16,32,512]{2,1,0:T(8,128)(2,1)}), bf16[16,32,512]{2,1,0:T(8,128)(2,1)S(1)}, u32[]{:S(2)}, u32[]{:S(2)}) async-start(bf16[16,32,512]{2,1,0:T(8,128)(2,1)} %bitcast.13), calls=%async_computation.1 | async-start | bytes 1048576 | tf_op jit(solution)/shard_map/all_to_all | solution.py:218
  159.2 35.0 %collective-permute-start.2 = (bf16[1024,256]{1,0:T(8,128)(2,1)S(1)}, bf16[1024,256]{1,0:T(8,128)(2,1)}, u32[]{:S(2)}, u32[]{:S(2)}) collective-permute-start(bf16[1024,256]{1,0:T(8,128)(2,1)S(1)} %maximum_select_fusion.1), channel_id=1, source_target_pairs={{0,4},{4,0},{1,5},{5,1},{2,6},{6,2},{3,7},{7,3},{8,12},{12,8},{9,1... | collective-permute-start | bytes 1572872 | tf_op jit(solution)/shard_map/ppermute | solution.py:26
  159.5 15.3 %collective-permute-start.5 = (bf16[128,1024]{1,0:T(8,128)(2,1)S(1)}, bf16[128,1024]{1,0:T(8,128)(2,1)S(1)}, u32[]{:S(2)}, u32[]{:S(2)}) collective-permute-start(bf16[128,1024]{1,0:T(8,128)(2,1)S(1)} %slice.44), channel_id=1, source_target_pairs={{0,64},{64,128},{128,192},{192,0},{1,65},{65,129},{129,193},{193,1... | collective-permute-start | bytes 786440 | tf_op jit(solution)/shard_map/ppermute | solution.py:193
  164.1 28.7 %copy-start.9 = (s32[8]{0:T(128)S(1)}, s32[8]{0:T(128)}, u32[]{:S(2)}) copy-start(s32[8]{0:T(128)} %param.9) | copy-start | bytes 100
  164.1 13.2 %collective-permute-start.6 = (bf16[128,1024]{1,0:T(8,128)(2,1)S(1)}, bf16[128,1024]{1,0:T(8,128)(2,1)S(1)}, u32[]{:S(2)}, u32[]{:S(2)}) collective-permute-start(bf16[128,1024]{1,0:T(8,128)(2,1)S(1)} %slice.45), channel_id=1, source_target_pairs={{0,192},{64,0},{128,64},{192,128},{1,193},{65,1},{129,65},{193,129... | collective-permute-start | bytes 786440 | tf_op jit(solution)/shard_map/ppermute | solution.py:194
  177.3 2.2 copy-start.1
  184.8 10.8 %copy-start.3 = (bf16[16,32,512]{2,1,0:T(8,128)(2,1)}, bf16[16,32,512]{2,1,0:T(8,128)(2,1)S(1)}, u32[]{:S(2)}) copy-start(bf16[16,32,512]{2,1,0:T(8,128)(2,1)S(1)} %all-to-all-done.1) | copy-start | bytes 1572868
  184.8 19.2 %all-to-all-start = ((bf16[16,32,512]{2,1,0:T(8,128)(2,1)}), bf16[16,32,512]{2,1,0:T(8,128)(2,1)}, u32[]{:S(2)}, u32[]{:S(2)}) async-start(bf16[16,32,512]{2,1,0:T(8,128)(2,1)} %bitcast.10), calls=%async_computation | async-start | bytes 1048576 | tf_op jit(solution)/shard_map/all_to_all | solution.py:218
  195.7 1.0 copy-start.4
  207.4 7.1 %collective-permute-start.18 = (bf16[2,272,256]{2,1,0:T(8,128)(2,1)S(1)}, bf16[2,272,256]{2,1,0:T(8,128)(2,1)S(1)}, u32[]{:S(2)}, u32[]{:S(2)}) collective-permute-start(bf16[2,272,256]{2,1,0:T(8,128)(2,1)S(1)} %get-tuple-element.20), channel_id=1, source_target_pairs={{0,2},{2,0},{1,3},{3,1},{4,6},{6,4},{5,7},{7,5},{8,10},{10,8},{9,1... | collective-permute-start | bytes 835592 | tf_op jit(solution)/shard_map/ppermute | solution.py:26
  207.5 7.4 %collective-permute-start.19 = (bf16[2,272,256]{2,1,0:T(8,128)(2,1)S(1)}, bf16[2,272,256]{2,1,0:T(8,128)(2,1)S(1)}, u32[]{:S(2)}, u32[]{:S(2)}) collective-permute-start(bf16[2,272,256]{2,1,0:T(8,128)(2,1)S(1)} %get-tuple-element.21), channel_id=1, source_target_pairs={{0,4},{4,0},{1,5},{5,1},{2,6},{6,2},{3,7},{7,3},{8,12},{12,8},{9,1... | collective-permute-start | bytes 835592 | tf_op jit(solution)/shard_map/ppermute | solution.py:26
  207.6 12.6 %collective-permute-start.20 = (bf16[2,272,256]{2,1,0:T(8,128)(2,1)S(1)}, bf16[2,272,256]{2,1,0:T(8,128)(2,1)S(1)}, u32[]{:S(2)}, u32[]{:S(2)}) collective-permute-start(bf16[2,272,256]{2,1,0:T(8,128)(2,1)S(1)} %get-tuple-element.22), channel_id=1, source_target_pairs={{0,6},{2,4},{4,2},{6,0},{1,7},{3,5},{5,3},{7,1},{8,14},{10,12},{12... | collective-permute-start | bytes 835592 | tf_op jit(solution)/shard_map/ppermute | solution.py:226
  221.2 6.3 %collective-permute-start.21 = (bf16[128,256]{1,0:T(8,128)(2,1)S(1)}, bf16[128,256]{1,0:T(8,128)(2,1)S(1)}, u32[]{:S(2)}, u32[]{:S(2)}) collective-permute-start(bf16[128,256]{1,0:T(8,128)(2,1)S(1)} %get-tuple-element.24), channel_id=1, source_target_pairs={{0,192},{64,0},{128,64},{192,128},{1,193},{65,1},{129,65},{193,129... | collective-permute-start | bytes 196616 | tf_op jit(solution)/shard_map/ppermute | solution.py:229
  223.8 7.7 %collective-permute-start.22 = (bf16[128,256]{1,0:T(8,128)(2,1)S(1)}, bf16[128,256]{1,0:T(8,128)(2,1)S(1)}, u32[]{:S(2)}, u32[]{:S(2)}) collective-permute-start(bf16[128,256]{1,0:T(8,128)(2,1)S(1)} %get-tuple-element.25), channel_id=1, source_target_pairs={{0,128},{64,192},{128,0},{192,64},{1,129},{65,193},{129,1},{193,65... | collective-permute-start | bytes 196616 | tf_op jit(solution)/shard_map/ppermute | solution.py:229
  227.5 5.7 %collective-permute-start.23 = (bf16[128,256]{1,0:T(8,128)(2,1)S(1)}, bf16[128,256]{1,0:T(8,128)(2,1)S(1)}, u32[]{:S(2)}, u32[]{:S(2)}) collective-permute-start(bf16[128,256]{1,0:T(8,128)(2,1)S(1)} %get-tuple-element.26), channel_id=1, source_target_pairs={{0,64},{64,128},{128,192},{192,0},{1,65},{65,129},{129,193},{193,1... | collective-permute-start | bytes 196616 | tf_op jit(solution)/shard_map/ppermute | solution.py:229
  233.3 3.4 %copy-start.2 = (bf16[1024,4096]{1,0:T(8,128)(2,1)S(1)}, bf16[1024,4096]{1,0:T(8,128)(2,1)}, u32[]{:S(2)}) copy-start(bf16[1024,4096]{1,0:T(8,128)(2,1)} %all-gather.5.cloned.1.call-done.refs_4_) | copy-start | bytes 25165828
  236.6 8.4 %copy-start.5 = (bf16[64,4096]{1,0:T(8,128)(2,1)S(1)}, bf16[64,4096]{1,0:T(8,128)(2,1)}, u32[]{:S(2)}) copy-start(bf16[64,4096]{1,0:T(8,128)(2,1)} %residual.1) | copy-start | bytes 1572868
  236.6 8.4 %copy-start.6 = (f32[4096]{0:T(1024)S(1)}, f32[4096]{0:T(1024)}, u32[]{:S(2)}) copy-start(f32[4096]{0:T(1024)} %param.13) | copy-start | bytes 49156
  238.5 6.6 %collective-permute-start.24 = (f32[64,4096]{1,0:T(8,128)S(1)}, f32[64,4096]{1,0:T(8,128)S(1)}, u32[]{:S(2)}, u32[]{:S(2)}) collective-permute-start(f32[64,4096]{1,0:T(8,128)S(1)} %get-tuple-element.29), channel_id=1, source_target_pairs={{0,1},{1,0},{2,3},{3,2},{4,5},{5,4},{6,7},{7,6},{8,9},{9,8},{10,11... | collective-permute-start | bytes 3145736 | tf_op jit(solution)/shard_map/ppermute | solution.py:26
Sparse Core Ops, SparseCore 0:
  17.3 57.8 all-gather.2
  77.6 80.7 all-gather.4
